TPU v7x, 32 devices: a whole 2x2x4 slice. The times are simulated.
32 devices in a mesh: dp: 16 (over z, x, core), seq: 2 (over y).
Axes of the slice: x: 2, y: 2, z: 4, core: 2. Of those that a mesh axis runs over, the one named last changes fastest.
Arguments:
- tokens: bfloat16 [16, 1152, 1024], P('dp', 'seq'), may hold values from -6 to 6
- w_qkv: bfloat16 [1024, 3072], P('dp'), may hold values from -0.1875 to 0.1875
- w_out: bfloat16 [1024, 1024], P('dp'), may hold values from -1 to 1
- w_up: bfloat16 [1024, 4096], P('dp'), may hold values from -0.1875 to 0.1875
- w_down: bfloat16 [4096, 1024], P('dp'), may hold values from -0.09375 to 0.09375
- gains: bfloat16 [1024, 2], P('dp'), may hold values from 0.5 to 1.5
- biases: bfloat16 [1024, 6], P('dp'), may hold values from -1.1953125 to 1.1953125
- up_bias: bfloat16 [4096], P('dp'), may hold values from -1.1953125 to 1.1953125
- valid: int32 [16], P('dp'), may hold values from 577 to 1152
- cotangent: bfloat16 [16, 1152, 1024], P('dp', 'seq'), may hold values from -6 to 6
Outputs:
- out_tokens: bfloat16 [16, 1152, 1024], P('dp', 'seq')
- grad_tokens: float32 [16, 1152, 1024], P('dp', 'seq')
- grad_qkv: float32 [1024, 3072], P('dp')
- grad_out: float32 [1024, 1024], P('dp')
- grad_up: float32 [1024, 4096], P('dp')
- grad_down: float32 [4096, 1024], P('dp')
- grad_gains: float32 [1024, 2], P('dp')
- grad_biases: float32 [1024, 6], P('dp')
- grad_up_bias: float32 [4096], P('dp')
Inputs may be any that keep to these rules, and one draw needn't show every extreme that they name: valid counts of the images; keys at positions from valid on are padding.
All inputs are finite; a program needn't handle non-finite values.
Results may differ from a plain program's by a relative error of at most 0.019.
Values may be sent and summed in bfloat16 or wider, within the bound.
A program may use at most 256 MiB of HBM per device.

v0:
```python
import jax
import jax.numpy as jnp
from jax import lax
from jax.sharding import PartitionSpec as P

HD = 64


EPSILON = 1e-06
NEG_FILL = -1e30


def layer_norm(values, scales, offset):
    average = jnp.mean(values, axis=-1, keepdims=True)
    centered = values - average
    variance = jnp.mean(centered * centered, axis=-1, keepdims=True)
    return centered * lax.rsqrt(variance + EPSILON) * scales + offset


def exact_gelu(values):
    return jax.nn.gelu(values, approximate=False)


def split_heads(block):
    seq_len = block.shape[0]
    return block.reshape(seq_len, block.shape[1] // HD, HD)


def score_block(query_heads, key_heads, length):
    scores = jnp.einsum("qhd,khd->hqk", query_heads, key_heads, preferred_element_type=jnp.float32)
    scores = scores * HD ** (-0.5)
    allowed = jnp.arange(key_heads.shape[0], dtype=jnp.int32) < length
    return jnp.where(allowed[None, None, :], scores, NEG_FILL)


def attend_forward(packed):
    queries, keyset, values, length = packed
    query_heads = split_heads(queries)
    key_heads = split_heads(keyset)
    value_heads = split_heads(values)
    scores = score_block(query_heads, key_heads, length)
    row_max = jnp.max(scores, axis=-1, keepdims=True)
    exp_scores = jnp.exp(scores - row_max)
    row_total = jnp.sum(exp_scores, axis=-1, keepdims=True)
    probs = (exp_scores / row_total).astype(jnp.bfloat16)
    result = jnp.einsum("hqk,khd->qhd", probs, value_heads, preferred_element_type=jnp.float32)
    log_total = row_max[..., 0] + jnp.log(row_total[..., 0])
    return (result.reshape(queries.shape).astype(jnp.bfloat16), log_total)


def attend_backward(packed):
    queries, keyset, values, length, log_total, grad_result = packed
    query_heads = split_heads(queries)
    key_heads = split_heads(keyset)
    value_heads = split_heads(values)
    grad_heads = split_heads(grad_result)
    scores = score_block(query_heads, key_heads, length)
    probs = jnp.exp(scores - log_total[:, :, None])
    grad_probs = jnp.einsum(
        "qhd,khd->hqk", grad_heads, value_heads, preferred_element_type=jnp.float32
    )
    row_delta = jnp.sum(probs * grad_probs, axis=-1, keepdims=True)
    grad_scores = (probs * (grad_probs - row_delta)).astype(jnp.bfloat16)
    grad_query = jnp.einsum(
        "hqk,khd->qhd", grad_scores, key_heads, preferred_element_type=jnp.float32
    ) * HD ** (-0.5)
    grad_key = jnp.einsum(
        "hqk,qhd->khd", grad_scores, query_heads, preferred_element_type=jnp.float32
    ) * HD ** (-0.5)
    grad_value = jnp.einsum(
        "hqk,qhd->khd", probs.astype(jnp.bfloat16), grad_heads, preferred_element_type=jnp.float32
    )
    flat_shape = queries.shape
    return (
        grad_query.reshape(flat_shape).astype(jnp.bfloat16),
        grad_key.reshape(flat_shape).astype(jnp.bfloat16),
        grad_value.reshape(flat_shape).astype(jnp.bfloat16),
    )


def per_device(tokens, w_qkv, w_out, w_up, w_down, gains, biases, up_bias, valid, cotangent):
    full_qkv, full_out, full_up, full_down, full_gains, full_biases, full_upb = (
        lax.all_gather(w_qkv, "dp", axis=0, tiled=True),
        lax.all_gather(w_out, "dp", axis=0, tiled=True),
        lax.all_gather(w_up, "dp", axis=0, tiled=True),
        lax.all_gather(w_down, "dp", axis=0, tiled=True),
        lax.all_gather(gains, "dp", axis=0, tiled=True),
        lax.all_gather(biases, "dp", axis=0, tiled=True),
        lax.all_gather(up_bias, "dp", axis=0, tiled=True),
    )
    gain_cols = full_gains.astype(jnp.float32)
    bias_cols = full_biases.astype(jnp.float32)
    upb_float = full_upb.astype(jnp.float32)
    images, local_len, model_width = tokens.shape
    token_shape = (images, local_len, model_width)
    flat_tokens = tokens.reshape(-1, model_width).astype(jnp.float32)
    normed_one, pull_one = jax.vjp(layer_norm, flat_tokens, gain_cols[:, 0], bias_cols[:, 0])
    first = normed_one.astype(jnp.bfloat16)
    mixed = jnp.dot(first, full_qkv, preferred_element_type=jnp.float32)
    queries = (mixed[:, :model_width] + bias_cols[:, 1]).astype(jnp.bfloat16)
    keyset = mixed[:, model_width : 2 * model_width].astype(jnp.bfloat16)
    values = (mixed[:, 2 * model_width :] + bias_cols[:, 2]).astype(jnp.bfloat16)
    head_q, head_k, head_v = (
        lax.all_to_all(
            queries.reshape(token_shape), "seq", split_axis=2, concat_axis=1, tiled=True
        ),
        lax.all_to_all(keyset.reshape(token_shape), "seq", split_axis=2, concat_axis=1, tiled=True),
        lax.all_to_all(values.reshape(token_shape), "seq", split_axis=2, concat_axis=1, tiled=True),
    )
    attended, log_totals = lax.map(attend_forward, (head_q, head_k, head_v, valid))
    back_tokens = lax.all_to_all(attended, "seq", split_axis=1, concat_axis=2, tiled=True)
    merged = back_tokens.reshape(-1, model_width)
    branch = jnp.dot(merged, full_out, preferred_element_type=jnp.float32) + bias_cols[:, 3]
    residual = flat_tokens + branch
    normed_two, pull_two = jax.vjp(layer_norm, residual, gain_cols[:, 1], bias_cols[:, 4])
    second = normed_two.astype(jnp.bfloat16)
    upward = jnp.dot(second, full_up, preferred_element_type=jnp.float32) + upb_float
    activated_float, pull_gelu = jax.vjp(exact_gelu, upward)
    activated = activated_float.astype(jnp.bfloat16)
    output = (
        residual
        + jnp.dot(activated, full_down, preferred_element_type=jnp.float32)
        + bias_cols[:, 5]
    )
    out_tokens = output.astype(jnp.bfloat16).reshape(token_shape)
    back_qkv, back_out, back_up, back_down = (full_qkv, full_out, full_up, full_down)
    grad_output = cotangent.reshape(-1, model_width)
    grad_down = jnp.dot(activated.T, grad_output, preferred_element_type=jnp.float32)
    grad_bias_down = jnp.sum(grad_output.astype(jnp.float32), axis=0)
    grad_act = jnp.dot(grad_output, back_down.T, preferred_element_type=jnp.float32)
    grad_upward = pull_gelu(grad_act)[0].astype(jnp.bfloat16)
    grad_up = jnp.dot(second.T, grad_upward, preferred_element_type=jnp.float32)
    grad_up_bias = jnp.sum(grad_upward.astype(jnp.float32), axis=0)
    grad_second = jnp.dot(grad_upward, back_up.T, preferred_element_type=jnp.float32)
    grad_resid_norm, grad_gain_two, grad_bias_two = pull_two(grad_second)
    grad_resid = grad_output.astype(jnp.float32) + grad_resid_norm
    grad_branch = grad_resid.astype(jnp.bfloat16)
    grad_out_weight = jnp.dot(merged.T, grad_branch, preferred_element_type=jnp.float32)
    grad_bias_out = jnp.sum(grad_branch.astype(jnp.float32), axis=0)
    grad_merged = jnp.dot(grad_branch, back_out.T, preferred_element_type=jnp.float32).astype(
        jnp.bfloat16
    )
    grad_head_result = lax.all_to_all(
        grad_merged.reshape(token_shape), "seq", split_axis=2, concat_axis=1, tiled=True
    )
    grad_q, grad_k, grad_v = lax.map(
        attend_backward, (head_q, head_k, head_v, valid, log_totals, grad_head_result)
    )
    tok_grad_q, tok_grad_k, tok_grad_v = (
        lax.all_to_all(grad_q, "seq", split_axis=1, concat_axis=2, tiled=True),
        lax.all_to_all(grad_k, "seq", split_axis=1, concat_axis=2, tiled=True),
        lax.all_to_all(grad_v, "seq", split_axis=1, concat_axis=2, tiled=True),
    )
    flat_grad_q = tok_grad_q.reshape(-1, model_width)
    flat_grad_v = tok_grad_v.reshape(-1, model_width)
    grad_mixed = jnp.concatenate(
        [flat_grad_q, tok_grad_k.reshape(-1, model_width), flat_grad_v], axis=1
    )
    grad_qkv = jnp.dot(first.T, grad_mixed, preferred_element_type=jnp.float32)
    grad_bias_q = jnp.sum(flat_grad_q.astype(jnp.float32), axis=0)
    grad_bias_v = jnp.sum(flat_grad_v.astype(jnp.float32), axis=0)
    grad_first = jnp.dot(grad_mixed, back_qkv.T, preferred_element_type=jnp.float32)
    grad_tok_norm, grad_gain_one, grad_bias_one = pull_one(grad_first)
    grad_tokens = (grad_resid + grad_tok_norm).reshape(token_shape)
    grad_gains = jnp.stack([grad_gain_one, grad_gain_two], axis=1)
    grad_biases = jnp.stack(
        [grad_bias_one, grad_bias_q, grad_bias_v, grad_bias_out, grad_bias_two, grad_bias_down],
        axis=1,
    )
    piece_qkv, piece_out, piece_up, piece_down, piece_gains, piece_biases, piece_upb = (
        lax.psum_scatter(
            grad_qkv.astype(jnp.bfloat16), "dp", scatter_dimension=0, tiled=True
        ).astype(jnp.float32),
        lax.psum_scatter(
            grad_out_weight.astype(jnp.bfloat16), "dp", scatter_dimension=0, tiled=True
        ).astype(jnp.float32),
        lax.psum_scatter(
            grad_up.astype(jnp.bfloat16), "dp", scatter_dimension=0, tiled=True
        ).astype(jnp.float32),
        lax.psum_scatter(
            grad_down.astype(jnp.bfloat16), "dp", scatter_dimension=0, tiled=True
        ).astype(jnp.float32),
        lax.psum_scatter(
            grad_gains.astype(jnp.bfloat16), "dp", scatter_dimension=0, tiled=True
        ).astype(jnp.float32),
        lax.psum_scatter(
            grad_biases.astype(jnp.bfloat16), "dp", scatter_dimension=0, tiled=True
        ).astype(jnp.float32),
        lax.psum_scatter(
            grad_up_bias.astype(jnp.bfloat16), "dp", scatter_dimension=0, tiled=True
        ).astype(jnp.float32),
    )
    totals = (
        lax.psum(piece_qkv.astype(jnp.bfloat16), "seq").astype(jnp.float32),
        lax.psum(piece_out.astype(jnp.bfloat16), "seq").astype(jnp.float32),
        lax.psum(piece_up.astype(jnp.bfloat16), "seq").astype(jnp.float32),
        lax.psum(piece_down.astype(jnp.bfloat16), "seq").astype(jnp.float32),
        lax.psum(piece_gains.astype(jnp.bfloat16), "seq").astype(jnp.float32),
        lax.psum(piece_biases.astype(jnp.bfloat16), "seq").astype(jnp.float32),
        lax.psum(piece_upb.astype(jnp.bfloat16), "seq").astype(jnp.float32),
    )
    return (
        out_tokens,
        grad_tokens,
        totals[0],
        totals[1],
        totals[2],
        totals[3],
        totals[4],
        totals[5],
        totals[6],
    )


def solution(mesh):
    return jax.shard_map(
        per_device,
        mesh=mesh,
        in_specs=(
            P("dp", "seq", None),
            P("dp", None),
            P("dp", None),
            P("dp", None),
            P("dp", None),
            P("dp", None),
            P("dp", None),
            P("dp"),
            P("dp"),
            P("dp", "seq", None),
        ),
        out_specs=(
            P("dp", "seq", None),
            P("dp", "seq", None),
            P("dp", None),
            P("dp", None),
            P("dp", None),
            P("dp", None),
            P("dp", None),
            P("dp", None),
            P("dp"),
        ),
        check_vma=False,
    )
```

profile of v0, /device:TPU:0, one launch (start us, length us, event | category | flops | bytes accessed | tf_op | source)
XLA Modules:
  0.0 1100.0 jit_solution(14046963542723650582)
XLA Ops:
  9.4 23.2 %all-gather = bf16[16,64,2]{1,2,0:T(2,128)(2,1)S(1)} all-gather(bf16[1,64,2]{1,2,0:T(2,128)(2,1)} %bitcast.251), channel_id=1, replica_groups=mesh['dp'=16,'seq'=2] {'dp'}, dimensions={0}, use_global_device_ids=true | all-gather | bytes 4352 | tf_op jit(solution)/shard_map/all_gather | solution.py:87
  32.7 17.9 %all-gather.1 = bf16[16,64,6]{1,2,0:T(8,128)(2,1)S(1)} all-gather(bf16[1,64,6]{1,2,0:T(8,128)(2,1)} %bitcast.250), channel_id=1, replica_groups=mesh['dp'=16,'seq'=2] {'dp'}, dimensions={0}, use_global_device_ids=true | all-gather | bytes 13056 | tf_op jit(solution)/shard_map/all_gather | solution.py:88
  53.4 21.5 %all-gather.8.cloned.1.call-done = bf16[1024,3072]{1,0:T(8,128)(2,1)} async-done(((bf16[64,3072]{1,0:T(8,128)(2,1)}), bf16[1024,3072]{1,0:T(8,128)(2,1)}) %all-gather.8.cloned.1.call-update) | async-done | bytes 6291472 | tf_op jit(solution)/shard_map/all_gather | solution.py:83
  208.8 16.1 %fusion.59 = (f32[8,1152]{1,0:T(8,128)S(1)}, f32[8,1152,1152]{1,2,0:T(8,128)}) fusion(bf16[1152,8,64]{0,2,1:T(8,128)(2,1)S(1)} %reshape.230, bf16[1152,8,64]{0,2,1:T(8,128)(2,1)S(1)} %reshape.232, pred[1152]{0:T(1024)(128)(4,1)S(1)} %iota_compare_fusion), kind=kOutput, calls=%fused_computation.104 | convolution fusion | flops 1390795776 | bytes 44864640 | tf_op jit(solution)/shard_map/while/body/eval_jaxpr/qhd,khd->hqk/dot_general | solution.py:30
  224.9 17.4 %fusion.1 = f32[8,1152]{1,0:T(8,128)S(1)} fusion(f32[8,1152,1152]{1,2,0:T(8,128)} %get-tuple-element.91, f32[8,1152]{1,0:T(8,128)S(1)} %get-tuple-element.90), kind=kLoop, calls=%fused_computation.7 | loop fusion | flops 21224448 | bytes 42541056 | tf_op jit(solution)/shard_map/while/body/eval_jaxpr/reduce_sum | solution.py:44
  242.4 18.1 %fusion.18 = bf16[8,64,1152]{2,1,0:T(8,128)(2,1)} fusion(bf16[1152,8,64]{0,2,1:T(8,128)(2,1)S(1)} %copy-done.17, f32[8,1152,1152]{1,2,0:T(8,128)} %get-tuple-element.91, f32[8,1152]{1,0:T(8,128)S(1)} %fusion.1, f32[8,1152]{1,0:T(8,128)S(1)} %get-tuple-element.90), kind=kOutput, calls=%fused_computation.39 | convolution fusion | flops 1391394816 | bytes 44900352 | tf_op jit(solution)/shard_map/while/body/eval_jaxpr/hqk,khd->qhd/dot_general | solution.py:46
  282.6 18.8 %all-gather.2 = bf16[16,1,256]{2,1,0:T(2,128)(2,1)S(1)} all-gather(bf16[1,1,256]{2,1,0:T(2,128)(2,1)S(1)} %reshape.246), channel_id=1, replica_groups=mesh['dp'=16,'seq'=2] {'dp'}, dimensions={0}, use_global_device_ids=true | all-gather | bytes 8704 | tf_op jit(solution)/shard_map/all_gather | solution.py:89
  310.8 30.8 %multiply_convert_fusion.1 = (bf16[576,4096]{1,0:T(8,128)(2,1)}, f32[576,4096]{1,0:T(8,128)}, f32[576,4096]{1,0:T(8,128)}) fusion(f32[4096]{0:T(1024)} %bitcast.240, bf16[1024,4096]{1,0:T(8,128)(2,1)} %all-gather.12.cloned.1.call-done, f32[576,1024]{1,0:T(8,128)S(1)} %get-tuple-element.93, f32[1024]{0:T(1024)} %bitcast.245, f32[1024]{0:T(1024)S(1)} %bitcast.234, ...), kind=kOutput, calls=%fused_computation.15 | convolution fusion | flops 4990500864 | bytes 34370048 | tf_op jit(solution)/shard_map/dot_general | solution.py:117
  341.7 15.7 %fusion.61 = (bf16[4096]{0:T(1024)(128)(2,1)}, bf16[576,4096]{1,0:T(8,128)(2,1)S(1)}) fusion(f32[576,4096]{1,0:T(8,128)} %get-tuple-element.79, bf16[4096,1024]{1,0:T(8,128)(2,1)} %all-gather.14.cloned.1.call-done, bf16[1,576,1024]{2,1,0:T(8,128)(2,1)S(1)} %copy-done.8, f32[576,4096]{1,0:T(8,128)} %get-tuple-element.94, f32[4096]{0:T(1024)} %bitcast.241), kind=kOutput, calls=%fused_computation.106 | convolution fusion | flops 4869582848 | bytes 33185792 | tf_op jit(solution)/shard_map/dot_general | solution.py:130
  357.4 10.7 multiply_reduce_fusion.1
  401.2 12.2 %all-to-all-done.4 = bf16[2,2,147456]{2,1,0:T(2,128)(2,1)} async-done(((bf16[2,2,147456]{2,1,0:T(2,128)(2,1)}), bf16[2,2,147456]{2,1,0:T(2,128)(2,1)}, u32[]{:S(2)}, u32[]{:S(2)}) %all-to-all-start.4) | async-done | bytes 1179680 | tf_op jit(solution)/shard_map/all_to_all | solution.py:143
  425.4 16.5 %fusion.15 = bf16[8,64,1152]{2,1,0:T(8,128)(2,1)S(1)} fusion(bf16[1152,8,64]{0,2,1:T(8,128)(2,1)S(1)} %reshape.237, f32[8,1152,1152]{1,2,0:T(8,128)} %get-tuple-element.91, f32[8,1152]{1,0:T(8,128)} %log_add_fusion), kind=kOutput, calls=%fused_computation.38 | convolution fusion | flops 1380777984 | bytes 44863488 | tf_op jit(solution)/shard_map/while/body/eval_jaxpr/hqk,qhd->khd/dot_general | solution.py:70
  442.0 32.1 %multiply_reduce_fusion = (f32[8,1152]{1,0:T(8,128)}, f32[8,1152,1152]{1,2,0:T(8,128)}) fusion(f32[8,1152,1152]{1,2,0:T(8,128)} %get-tuple-element.91, f32[8,1152]{1,0:T(8,128)} %log_add_fusion, bf16[1152,8,64]{0,2,1:T(8,128)(2,1)S(1)} %reshape.237, bf16[1152,8,64]{0,2,1:T(8,128)(2,1)S(1)} %copy-done.18), kind=kOutput, calls=%fused_computation.3 | convolution fusion | flops 1390795776 | bytes 87367680 | tf_op jit(solution)/shard_map/while/body/eval_jaxpr/qhd,khd->hqk/dot_general | solution.py:59
  492.1 34.8 %multiply_convert_fusion = bf16[8,1152,1152]{1,2,0:T(8,128)(2,1)} fusion(f32[8,1152,1152]{1,2,0:T(8,128)} %get-tuple-element.97, f32[8,1152,1152]{1,2,0:T(8,128)} %get-tuple-element.91, f32[8,1152]{1,0:T(8,128)S(1)} %copy-done.27, f32[8,1152]{1,0:T(8,128)S(1)} %copy-done.19), kind=kLoop, calls=%fused_computation.2 | loop fusion | flops 42467328 | bytes 106242048 | tf_op jit(solution)/shard_map/while/body/eval_jaxpr/convert_element_type | solution.py:63
  526.9 10.7 fusion.14
  555.7 10.5 fusion.13
  615.3 12.2 %convolution_convert_fusion = bf16[1024,4096]{1,0:T(8,128)(2,1)} fusion(bf16[576,4096]{1,0:T(8,128)(2,1)} %copy-done.49, f32[576,1024]{1,0:T(8,128)} %copy-done.10, f32[1024]{0:T(1024)} %bitcast.246, f32[1024]{0:T(1024)} %bitcast.237, f32[576]{0:T(1024)} %copy-done.40, f32[576]{0:T(1024)S(1)} %broadcast_multiply_fusion), kind=kOutput, calls=%fused_computation.29 | convolution fusion | flops 4838981632 | bytes 15479296 | tf_op jit(solution)/shard_map/dot_general | solution.py:132
  627.6 11.2 %convolution_convert_fusion.1 = bf16[4096,1024]{1,0:T(8,128)(2,1)} fusion(bf16[576,4096]{1,0:T(8,128)(2,1)} %get-tuple-element.78, bf16[1,576,1024]{2,1,0:T(8,128)(2,1)} %param.19), kind=kOutput, calls=%fused_computation.30 | convolution fusion | flops 4836032512 | bytes 14286848 | tf_op jit(solution)/shard_map/dot_general | solution.py:128
  664.7 31.7 %all-reduce = bf16[4096]{0:T(1024)(128)(2,1)S(1)} all-reduce(bf16[4096]{0:T(1024)(128)(2,1)} %get-tuple-element.99), channel_id=8, replica_groups=mesh['dp'=16,'seq'=2] {'dp'}, use_global_device_ids=true, to_apply=%region_32.33.clone | all-reduce | flops 4096 | bytes 16384
  698.9 107.8 %reduce-scatter.15.cloned.1.call-done = bf16[64,4096]{1,0:T(8,128)(2,1)} async-done(((bf16[1024,4096]{1,0:T(8,128)(2,1)}), bf16[64,4096]{1,0:T(8,128)(2,1)}) %reduce-scatter.15.cloned.1.call-update) | async-done | bytes 524304 | tf_op jit(solution)/shard_map/reduce_scatter | solution.py:177
  806.6 108.5 %reduce-scatter.17.cloned.1.call-done = bf16[256,1024]{1,0:T(8,128)(2,1)} async-done(((bf16[4096,1024]{1,0:T(8,128)(2,1)}), bf16[256,1024]{1,0:T(8,128)(2,1)}) %reduce-scatter.17.cloned.1.call-update) | async-done | bytes 524304 | tf_op jit(solution)/shard_map/reduce_scatter | solution.py:180
  927.9 46.4 %reduce-scatter.19.cloned.1.call-done = bf16[64,2]{1,0:T(8,128)(2,1)} async-done(((bf16[1024,2]{1,0:T(8,128)(2,1)}), bf16[64,2]{1,0:T(8,128)(2,1)}) %reduce-scatter.19.cloned.1.call-update) | async-done | bytes 272
  975.1 57.5 %reduce-scatter.21.cloned.1.call-done = bf16[64,6]{1,0:T(8,128)(2,1)} async-done(((bf16[1024,6]{1,0:T(8,128)(2,1)}), bf16[64,6]{1,0:T(8,128)(2,1)}) %reduce-scatter.21.cloned.1.call-update) | async-done | bytes 784
  1040.0 46.1 %all-reduce.5.cloned.1.call-done = (bf16[64,3072]{1,0:T(8,128)(2,1)}, bf16[64,1024]{1,0:T(8,128)(2,1)}, bf16[64,4096]{1,0:T(8,128)(2,1)}, bf16[256,1024]{1,0:T(8,128)(2,1)}) async-done(((bf16[64,3072]{1,0:T(8,128)(2,1)}, bf16[64,1024]{1,0:T(8,128)(2,1)}, bf16[64,4096]{1,0:T(8,128)(2,1)}, bf16[256,1024]{1,0:T(8,128)(2,1)}), (bf16[64,3072]{1,0:T(8,128)(2,1)}, bf16[64,1024]{1,0:T(8,128)(2,1)}, ...) | async-done | bytes 1572880 | tf_op jit(solution)/shard_map/psum | solution.py:194
  (267 shorter events, 355.1 us)
Async XLA Ops:
  7.2 45.0 %copy-start.2 = (bf16[1,576,1024]{2,1,0:T(8,128)(2,1)S(1)}, bf16[1,576,1024]{2,1,0:T(8,128)(2,1)}, u32[]{:S(2)}) copy-start(bf16[1,576,1024]{2,1,0:T(8,128)(2,1)} %param.10) | copy-start | bytes 3538948
  7.2 67.7 %all-gather.8.cloned.1.call-start = ((), (), s32[]{:S(2)}) async-start(), calls=%async_computation.14 | async-start | bytes 6684672 | tf_op jit(solution)/shard_map/all_gather | solution.py:83
  7.9 299.0 %all-gather.10.cloned.1.call-start = ((), (), s32[]{:S(2)}) async-start(), calls=%async_computation.15 | async-start | bytes 2228224 | tf_op jit(solution)/shard_map/all_gather | solution.py:84
  8.7 302.1 %all-gather.12.cloned.1.call-start = ((), (), s32[]{:S(2)}) async-start(), calls=%async_computation.16 | async-start | bytes 8912896 | tf_op jit(solution)/shard_map/all_gather | solution.py:85
  52.7 315.3 %copy-start.41 = (f32[1024,1]{0,1:T(1,128)}, f32[1024,1]{0,1:T(1,128)S(1)}, u32[]{:S(2)}) copy-start(f32[1024,1]{0,1:T(1,128)S(1)} %get-tuple-element.88) | copy-start | bytes 12292
  101.3 23.0 %all-to-all-start.1 = ((bf16[2,2,147456]{2,1,0:T(2,128)(2,1)}), bf16[2,2,147456]{2,1,0:T(2,128)(2,1)}, u32[]{:S(2)}, u32[]{:S(2)}) async-start(bf16[2,2,147456]{2,1,0:T(2,128)(2,1)} %reshape.262), calls=%async_computation.1 | async-start | bytes 2359296 | tf_op jit(solution)/shard_map/all_to_all | solution.py:104
  124.3 21.5 %all-to-all-start.2 = ((bf16[2,2,147456]{2,1,0:T(2,128)(2,1)}), bf16[2,2,147456]{2,1,0:T(2,128)(2,1)}, u32[]{:S(2)}, u32[]{:S(2)}) async-start(bf16[2,2,147456]{2,1,0:T(2,128)(2,1)} %reshape.264), calls=%async_computation.2 | async-start | bytes 2359296 | tf_op jit(solution)/shard_map/all_to_all | solution.py:107
  145.8 41.7 %all-to-all-start = ((bf16[2,2,147456]{2,1,0:T(2,128)(2,1)}), bf16[2,2,147456]{2,1,0:T(2,128)(2,1)}, u32[]{:S(2)}, u32[]{:S(2)}) async-start(bf16[2,2,147456]{2,1,0:T(2,128)(2,1)} %reshape.260), calls=%async_computation | async-start | bytes 2359296 | tf_op jit(solution)/shard_map/all_to_all | solution.py:108
  150.3 191.4 %all-gather.14.cloned.1.call-start = ((), (), s32[]{:S(2)}) async-start(), calls=%async_computation.17 | async-start | bytes 8912896 | tf_op jit(solution)/shard_map/all_gather | solution.py:86
  278.1 23.9 %all-to-all-start.3 = ((bf16[2,2,147456]{2,1,0:T(2,128)(2,1)}), bf16[2,2,147456]{2,1,0:T(2,128)(2,1)}, u32[]{:S(2)}, u32[]{:S(2)}) async-start(bf16[2,2,147456]{2,1,0:T(2,128)(2,1)} %reshape.266), calls=%async_computation.3 | async-start | bytes 2359296 | tf_op jit(solution)/shard_map/all_to_all | solution.py:111
  310.4 57.7 %copy-start.10 = (f32[576,1024]{1,0:T(8,128)}, f32[576,1024]{1,0:T(8,128)S(1)}, u32[]{:S(2)}) copy-start(f32[576,1024]{1,0:T(8,128)S(1)} %get-tuple-element.93) | copy-start | bytes 7077892
  310.8 57.3 %copy-start.40 = (f32[576]{0:T(1024)}, f32[576]{0:T(1024)S(1)}, u32[]{:S(2)}) copy-start(f32[576]{0:T(1024)S(1)} %fusion.46) | copy-start | bytes 6916
  392.8 20.6 %all-to-all-start.4 = ((bf16[2,2,147456]{2,1,0:T(2,128)(2,1)}), bf16[2,2,147456]{2,1,0:T(2,128)(2,1)}, u32[]{:S(2)}, u32[]{:S(2)}) async-start(bf16[2,2,147456]{2,1,0:T(2,128)(2,1)} %reshape.268), calls=%async_computation.4 | async-start | bytes 2359296 | tf_op jit(solution)/shard_map/all_to_all | solution.py:143
  397.3 299.1 %reduce-scatter.13.cloned.1.call-start = ((), (), s32[]{:S(2)}) async-start(), calls=%async_computation.19 | async-start | bytes 2228224 | tf_op jit(solution)/shard_map/reduce_scatter | solution.py:174
  487.6 63.7 %all-to-all-start.7 = ((bf16[2,2,147456]{2,1,0:T(2,128)(2,1)}), bf16[2,2,147456]{2,1,0:T(2,128)(2,1)}, u32[]{:S(2)}, u32[]{:S(2)}) async-start(bf16[2,2,147456]{2,1,0:T(2,128)(2,1)} %reshape.274), calls=%async_computation.7 | async-start | bytes 2359296 | tf_op jit(solution)/shard_map/all_to_all | solution.py:152
  551.2 28.5 %all-to-all-start.6 = ((bf16[2,2,147456]{2,1,0:T(2,128)(2,1)}), bf16[2,2,147456]{2,1,0:T(2,128)(2,1)}, u32[]{:S(2)}, u32[]{:S(2)}) async-start(bf16[2,2,147456]{2,1,0:T(2,128)(2,1)} %reshape.272), calls=%async_computation.6 | async-start | bytes 2359296 | tf_op jit(solution)/shard_map/all_to_all | solution.py:151
  579.8 19.1 %all-to-all-start.5 = ((bf16[2,2,147456]{2,1,0:T(2,128)(2,1)}), bf16[2,2,147456]{2,1,0:T(2,128)(2,1)S(1)}, u32[]{:S(2)}, u32[]{:S(2)}) async-start(bf16[2,2,147456]{2,1,0:T(2,128)(2,1)} %reshape.270), calls=%async_computation.5 | async-start | bytes 2359296 | tf_op jit(solution)/shard_map/all_to_all | solution.py:150
  583.4 115.5 %reduce-scatter.11.cloned.1.call-start = ((), (), s32[]{:S(2)}) async-start(), calls=%async_computation.18 | async-start | bytes 6684672 | tf_op jit(solution)/shard_map/reduce_scatter | solution.py:171
  615.3 191.4 %reduce-scatter.15.cloned.1.call-start = ((), (), s32[]{:S(2)}) async-start(), calls=%async_computation.20 | async-start | bytes 8912896 | tf_op jit(solution)/shard_map/reduce_scatter | solution.py:177
  627.5 287.6 %reduce-scatter.17.cloned.1.call-start = ((), (), s32[]{:S(2)}) async-start(), calls=%async_computation.21 | async-start | bytes 8912896 | tf_op jit(solution)/shard_map/reduce_scatter | solution.py:180
  638.8 335.5 %reduce-scatter.19.cloned.1.call-start = ((), (), s32[]{:S(2)}) async-start(), calls=%async_computation.22 | async-start | bytes 278528
  652.7 379.9 %reduce-scatter.21.cloned.1.call-start = ((), (), s32[]{:S(2)}) async-start(), calls=%async_computation.23 | async-start | bytes 278528
  659.5 255.7 %copy-start.43 = (f32[1024,1]{0,1:T(1,128)S(1)}, f32[1024,1]{0,1:T(1,128)}, u32[]{:S(2)}) copy-start(f32[1024,1]{0,1:T(1,128)} %get-tuple-element.82) | copy-start | bytes 12292
  662.7 423.5 %all-reduce.5.cloned.1.call-start = ((), (), s32[]{:S(2)}) async-start(), calls=%async_computation.24 | async-start | bytes 3145728 | tf_op jit(solution)/shard_map/psum | solution.py:194
  (45 other events, 507.2 us)
Sparse Core Ops, SparseCore 0:
  10.3 64.5 all-gather.7
  77.1 40.0 all-gather.9
  119.4 73.6 all-gather.11
  195.1 73.1 all-gather.13
  401.6 59.3 reduce-scatter.12
  615.4 83.4 reduce-scatter.10
  702.9 103.6 reduce-scatter.14
  810.7 104.3 reduce-scatter.16
  919.2 55.0 reduce-scatter.18
  978.2 54.3 reduce-scatter.20
  1035.1 51.0 all-reduce.4
where the time goes:
time: 1110 us; the launch traced here: 1100 us
  waiting for transfers between devices  405 us (36%)
  matrix products  226 us (20%)
  local copies, waits for them, and re-layouts  173 us (16%)
  other arithmetic  147 us (13%)
  blocking collectives  96.4 us (9%)
  starting transfers between devices  35.5 us (3%)
  between operations  16.6 us (1%)
    reduce_scatter x1, waiting for transfers between devices, per_device(): lax.psum_scatter(grad_down.astype(jnp.bfloat16), 'dp', scatter_dimension=...  108 us
    reduce_scatter x1, waiting for transfers between devices, per_device(): lax.psum_scatter(grad_up.astype(jnp.bfloat16), 'dp', scatter_dimension=0,...  108 us
    unnamed x13, waiting for transfers between devices  107 us
    unnamed x140, local copies, waits for them, and re-layouts  80.5 us
    unnamed x8, other arithmetic  71.4 us
    psum x1, waiting for transfers between devices, per_device(): lax.psum(piece_qkv.astype(jnp.bfloat16), 'seq').astype(jnp.float32)  46.1 us
    convert_element_type x1, other arithmetic, attend_backward(): grad_scores = (probs * (grad_probs - row_delta)).astype(jnp.bfloat16)  34.8 us
    dot_general x1, matrix products, attend_backward(): jnp.einsum('qhd,khd->hqk', grad_heads, value_heads, preferred_element_typ...  32.1 us
  transfers between devices with their start and end apart: 19, of which 8 were waited for; matrix products, arithmetic and copies ran while one was open for 44% of the time, Pallas kernels for 0%

commit v1 on v0

v1 whole, which is shorter than its diff:
```python
import functools

import jax
import jax.numpy as jnp
from jax import lax
from jax.experimental import pallas as pl
from jax.experimental.pallas import tpu as pltpu
from jax.sharding import PartitionSpec as P

HD = 64
PAIR = 2 * HD
EPSILON = 1e-06
NEG_FILL = -1e30
SMALL = 128
SPLITS = 2


def layer_norm(values, scales, offset):
    average = jnp.mean(values, axis=-1, keepdims=True)
    centered = values - average
    variance = jnp.mean(centered * centered, axis=-1, keepdims=True)
    return centered * lax.rsqrt(variance + EPSILON) * scales + offset


def dot_f32(a, b, dims):
    return lax.dot_general(a, b, (dims, ((), ())), preferred_element_type=jnp.float32)


def head_masks(dtype):
    lane = lax.broadcasted_iota(jnp.int32, (1, PAIR), 1)
    return (lane < HD).astype(dtype), (lane >= HD).astype(dtype)


def allowed_keys(place_ref, valid_ref, length, shards):
    row = lax.broadcasted_iota(jnp.int32, (shards * length, 1), 0)
    position = row + place_ref[0] * length
    position = jnp.where(position >= shards * length, position - shards * length, position)
    return position < valid_ref[pl.program_id(0)]


def stacked(refs):
    return jnp.concatenate([ref[...] for ref in refs], axis=0)


def forward_kernel(shards, place_ref, valid_ref, q_ref, *refs):
    k_refs, v_refs, (out_ref, lse_ref) = refs[:shards], refs[shards : 2 * shards], refs[2 * shards :]
    allowed = allowed_keys(place_ref, valid_ref, q_ref.shape[0], shards)
    keys, values = stacked(k_refs), stacked(v_refs)
    queries = q_ref[...] * jnp.bfloat16(HD**-0.5)
    total = None
    for head, mask in enumerate(head_masks(jnp.bfloat16)):
        scores = dot_f32(keys, queries * mask, ((1,), (1,)))
        scores = jnp.where(allowed, scores, NEG_FILL)
        top = jnp.max(scores, axis=0, keepdims=True)
        weight = jnp.exp(scores - top)
        row_total = jnp.sum(weight, axis=0, keepdims=True)
        part = dot_f32(values * mask, weight.astype(jnp.bfloat16), ((0,), (0,)))
        part = part / row_total
        total = part if total is None else total + part
        lse_ref[0, 0, head : head + 1, :] = top + jnp.log(row_total)
    out_ref[...] = total.T.astype(out_ref.dtype)


def backward_kernel(shards, place_ref, valid_ref, q_ref, *refs):
    k_refs, v_refs, refs = refs[:shards], refs[shards : 2 * shards], refs[2 * shards :]
    lse_ref, da_ref, dq_ref = refs[:3]
    dk_refs, dv_refs = refs[3 : 3 + shards], refs[3 + shards :]
    length = q_ref.shape[0]
    allowed = allowed_keys(place_ref, valid_ref, length, shards)
    keys, values = stacked(k_refs), stacked(v_refs)
    queries = q_ref[...] * jnp.bfloat16(HD**-0.5)
    grads = da_ref[...]
    dq = dk = dv = None
    for head, mask in enumerate(head_masks(jnp.bfloat16)):
        own_q = queries * mask
        own_g = grads * mask
        scores = dot_f32(keys, own_q, ((1,), (1,)))
        scores = jnp.where(allowed, scores, NEG_FILL)
        probs = jnp.exp(scores - lse_ref[0, 0, head : head + 1, :])
        dprobs = dot_f32(values, own_g, ((1,), (1,)))
        delta = jnp.sum(probs * dprobs, axis=0, keepdims=True)
        dscores = (probs * (dprobs - delta)).astype(jnp.bfloat16)
        part_v = dot_f32(probs.astype(jnp.bfloat16), own_g, ((1,), (0,)))
        part_k = dot_f32(dscores, own_q, ((1,), (0,)))
        part_q = dot_f32(keys * mask, dscores, ((0,), (0,)))
        dq = part_q if dq is None else dq + part_q
        dk = part_k if dk is None else dk + part_k
        dv = part_v if dv is None else dv + part_v
    dq_ref[...] = (dq * HD**-0.5).T.astype(dq_ref.dtype)
    for j in range(shards):
        rows = slice(j * length, (j + 1) * length)
        dk_refs[j][...] = dk[rows].astype(dk_refs[j].dtype)
        dv_refs[j][...] = dv[rows].astype(dv_refs[j].dtype)


def attention_specs(length):
    smem = pl.BlockSpec(memory_space=pltpu.SMEM)
    block = pl.BlockSpec((length, PAIR), lambda i, h: (i, h))
    lse = pl.BlockSpec((1, 1, 2, length), lambda i, h: (i, h, 0, 0))
    return smem, block, lse


def attend_forward(images, place, valid, q, keys, values):
    shards = len(keys)
    rows, width = q.shape
    length, pairs = rows // images, width // PAIR
    smem, block, lse = attention_specs(length)
    return pl.pallas_call(
        functools.partial(forward_kernel, shards),
        grid=(images, pairs),
        in_specs=[smem, smem] + [block] * (1 + 2 * shards),
        out_specs=[block, lse],
        out_shape=[
            jax.ShapeDtypeStruct((rows, width), jnp.bfloat16),
            jax.ShapeDtypeStruct((images, pairs, 2, length), jnp.float32),
        ],
        compiler_params=pltpu.CompilerParams(vmem_limit_bytes=40 * 2**20),
        cost_estimate=pl.CostEstimate(
            flops=8 * shards * rows * length * width, bytes_accessed=12 * rows * width,
            transcendentals=shards * rows * length * width // HD,
        ),
    )(place, valid, q, *keys, *values)


def attend_backward(images, place, valid, q, keys, values, lse_in, da):
    shards = len(keys)
    rows, width = q.shape
    length, pairs = rows // images, width // PAIR
    smem, block, lse = attention_specs(length)
    low = jax.ShapeDtypeStruct((rows, width), jnp.bfloat16)
    wide = jax.ShapeDtypeStruct((rows, width), jnp.float32)
    return pl.pallas_call(
        functools.partial(backward_kernel, shards),
        grid=(images, pairs),
        in_specs=[smem, smem] + [block] * (1 + 2 * shards) + [lse, block],
        out_specs=[block] * (1 + 2 * shards),
        out_shape=[low] + 2 * ([wide] + [low] * (shards - 1)),
        compiler_params=pltpu.CompilerParams(vmem_limit_bytes=48 * 2**20),
        cost_estimate=pl.CostEstimate(
            flops=20 * shards * rows * length * width, bytes_accessed=26 * rows * width,
            transcendentals=shards * rows * length * width // HD,
        ),
    )(place, valid, q, *keys, *values, lse_in, da)


def shift(values, shards, step):
    return lax.ppermute(values, "seq", [(i, (i + step) % shards) for i in range(shards)])


def per_device(tokens, w_qkv, w_out, w_up, w_down, gains, biases, up_bias, valid, cotangent):
    images, local_len, width = tokens.shape
    shard_rows = w_qkv.shape[0]
    ups = up_bias.shape[0] // shard_rows
    hidden = w_up.shape[1]
    token_shape = tokens.shape
    shards = lax.axis_size("seq")
    place = lax.axis_index("seq").astype(jnp.int32).reshape(1)

    gather = functools.partial(lax.all_gather, axis_name="dp", axis=0, tiled=True)
    scatter = functools.partial(
        lax.psum_scatter, axis_name="dp", scatter_dimension=0, tiled=True
    )
    smalls = jnp.concatenate([gains, biases, up_bias.reshape(shard_rows, ups)], axis=1)
    smalls = jnp.pad(smalls, ((0, 0), (0, SMALL - smalls.shape[1])))
    full_qkvs = gather(jnp.concatenate([w_qkv, smalls], axis=1))
    out_up = jnp.concatenate([w_out, w_up], axis=1)
    out_up, full_qkvs = lax.optimization_barrier((out_up, full_qkvs))
    full_out_up = gather(out_up)
    w_down, full_out_up = lax.optimization_barrier((w_down, full_out_up))
    full_down = gather(w_down)

    full_qkv = full_qkvs[:, : 3 * width]
    small = full_qkvs[:, 3 * width :].astype(jnp.float32).T
    gain_one, gain_two = small[0], small[1]
    bias_one, bias_q, bias_v, bias_out, bias_two, bias_down = (small[2 + i] for i in range(6))
    bias_up = small[8 : 8 + ups].T.reshape(-1)
    full_out = full_out_up[:, :width]
    full_up = full_out_up[:, width:]

    flat_tokens = tokens.reshape(-1, width).astype(jnp.float32)
    normed_one, pull_one = jax.vjp(layer_norm, flat_tokens, gain_one, bias_one)
    first = normed_one.astype(jnp.bfloat16)

    piece = width // SPLITS
    groups = []
    for g in range(SPLITS):
        lo, hi = g * piece, (g + 1) * piece
        k = jnp.dot(
            first, full_qkv[:, width + lo : width + hi], preferred_element_type=jnp.float32
        ).astype(jnp.bfloat16)
        v = jnp.dot(
            first, full_qkv[:, 2 * width + lo : 2 * width + hi],
            preferred_element_type=jnp.float32,
        )
        v = (v + bias_v[lo:hi]).astype(jnp.bfloat16)
        q = jnp.dot(first, full_qkv[:, lo:hi], preferred_element_type=jnp.float32)
        q = (q + bias_q[lo:hi]).astype(jnp.bfloat16)
        keys = [k] + [shift(k, shards, -j) for j in range(1, shards)]
        values = [v] + [shift(v, shards, -j) for j in range(1, shards)]
        groups.append((q, keys, values))
    parts = [attend_forward(images, place, valid, *group) for group in groups]
    merged = jnp.concatenate([part[0] for part in parts], axis=1)

    branch = jnp.dot(merged, full_out, preferred_element_type=jnp.float32) + bias_out
    residual = flat_tokens + branch
    normed_two, pull_two = jax.vjp(layer_norm, residual, gain_two, bias_two)
    second = normed_two.astype(jnp.bfloat16)
    upward = jnp.dot(second, full_up, preferred_element_type=jnp.float32) + bias_up
    cdf = 0.5 * (1.0 + lax.erf(upward * 0.5**0.5))
    activated = (upward * cdf).astype(jnp.bfloat16)
    slope = cdf + upward * (jnp.exp(-0.5 * upward * upward) * 0.3989422804014327)
    slope = slope.astype(jnp.bfloat16)

    grad_output = cotangent.reshape(-1, width)
    grad_down = dot_f32(activated, grad_output, ((0,), (0,))).astype(jnp.bfloat16)
    grad_down, full_down, activated = lax.optimization_barrier((grad_down, full_down, activated))
    piece_down = scatter(grad_down)

    grad_act = dot_f32(grad_output, full_down, ((1,), (1,)))
    grad_upward = (grad_act * slope.astype(jnp.float32)).astype(jnp.bfloat16)
    grad_second = dot_f32(grad_upward, full_up, ((1,), (1,)))
    grad_resid_norm, grad_gain_two, grad_bias_two = pull_two(grad_second)
    grad_resid = grad_output.astype(jnp.float32) + grad_resid_norm
    grad_branch = grad_resid.astype(jnp.bfloat16)
    grad_merged = dot_f32(grad_branch, full_out, ((1,), (1,))).astype(jnp.bfloat16)
    grad_up = dot_f32(second, grad_upward, ((0,), (0,))).astype(jnp.bfloat16)
    grad_out_weight = dot_f32(merged, grad_branch, ((0,), (0,))).astype(jnp.bfloat16)
    grad_out_up = jnp.concatenate([grad_out_weight, grad_up], axis=1)
    grad_out_up, grad_merged = lax.optimization_barrier((grad_out_up, grad_merged))
    piece_out_up = scatter(grad_out_up)

    backs = []
    for g, (group, part) in enumerate(zip(groups, parts)):
        lo, hi = g * piece, (g + 1) * piece
        grads = grad_merged[:, lo:hi]
        if g == SPLITS - 1:
            grads, piece_down = lax.optimization_barrier((grads, piece_down))
        dq, *rest = attend_backward(images, place, valid, *group, part[1], grads)
        dk, dv = rest[0], rest[shards]
        for j in range(1, shards):
            dk = dk + shift(rest[j], shards, j).astype(jnp.float32)
            dv = dv + shift(rest[shards + j], shards, j).astype(jnp.float32)
        dk, dv = dk.astype(jnp.bfloat16), dv.astype(jnp.bfloat16)
        backs.append((dq, dk, dv))
    grad_mixed = jnp.concatenate(
        [back[part] for part in range(3) for back in backs], axis=1
    )
    grad_qkv = dot_f32(first, grad_mixed, ((0,), (0,))).astype(jnp.bfloat16)
    grad_first = dot_f32(grad_mixed, full_qkv, ((1,), (1,)))
    grad_tok_norm, grad_gain_one, grad_bias_one = pull_one(grad_first)
    grad_tokens = (grad_resid + grad_tok_norm).reshape(token_shape)

    def token_sum(values):
        return jnp.sum(values.astype(jnp.float32), axis=0)

    small_grads = jnp.stack(
        [
            grad_gain_one, grad_gain_two, grad_bias_one,
            token_sum(grad_mixed[:, :width]), token_sum(grad_mixed[:, 2 * width :]),
            token_sum(grad_branch), grad_bias_two, token_sum(grad_output),
        ],
        axis=1,
    )
    small_grads = jnp.concatenate([small_grads, token_sum(grad_upward).reshape(width, -1)], axis=1)
    small_grads = jnp.pad(small_grads, ((0, 0), (0, SMALL - small_grads.shape[1])))
    grad_qkvs = jnp.concatenate([grad_qkv, small_grads.astype(jnp.bfloat16)], axis=1)
    grad_qkvs, piece_out_up = lax.optimization_barrier((grad_qkvs, piece_out_up))
    piece_qkvs = scatter(grad_qkvs)

    output = residual + jnp.dot(activated, full_down, preferred_element_type=jnp.float32)
    out_tokens = (output + bias_down).astype(jnp.bfloat16).reshape(token_shape)

    def both(values):
        if shards == 2:
            return values.astype(jnp.float32) + shift(values, shards, 1).astype(jnp.float32)
        return lax.psum(values, "seq").astype(jnp.float32)

    total_down, total_out_up, total_qkvs = both(piece_down), both(piece_out_up), both(piece_qkvs)
    total_small = total_qkvs[:, 3 * width :]
    return (
        out_tokens,
        grad_tokens,
        total_qkvs[:, : 3 * width],
        total_out_up[:, :width],
        total_out_up[:, width:],
        total_down,
        total_small[:, :2],
        total_small[:, 2:8],
        total_small[:, 8 : 8 + ups].reshape(-1),
    )


def solution(mesh):
    return jax.shard_map(
        per_device,
        mesh=mesh,
        in_specs=(
            P("dp", "seq", None),
            P("dp", None),
            P("dp", None),
            P("dp", None),
            P("dp", None),
            P("dp", None),
            P("dp", None),
            P("dp"),
            P("dp"),
            P("dp", "seq", None),
        ),
        out_specs=(
            P("dp", "seq", None),
            P("dp", "seq", None),
            P("dp", None),
            P("dp", None),
            P("dp", None),
            P("dp", None),
            P("dp", None),
            P("dp", None),
            P("dp"),
        ),
        check_vma=False,
    )
```

time: 1110 us -> 605 us (0.55)
  local copies, waits for them, and re-layouts: 173 us -> 38.7 us
  matrix products: 226 us -> 99.9 us
  other arithmetic: 147 us -> 26.6 us
  blocking collectives: 96.4 us -> 0 us
  waiting for transfers between devices: 405 us -> 338 us
  Pallas kernels: 0 us -> 65.1 us
  starting transfers between devices: 35.5 us -> 13.1 us
    all_gather x4 -> x3, waiting for transfers between devices: 21.6 us -> 154 us  [the longest x1 89.3 us: per_device(): full_out_up = gather(out_up)]
    dot_general x17 -> x16, matrix products: 215 us -> 90 us  [the longest x8 66.2 us: dot_f32(): lax.dot_general(a, b, (dims, ((), ())), preferred_element_type=jnp.float32)]
    unnamed x13 -> x6, waiting for transfers between devices: 107 us -> 0.1 us
    reduce_scatter x4 -> x3, waiting for transfers between devices: 219 us -> 134 us  [the longest x1 71.8 us: per_device(): piece_qkvs = scatter(grad_qkvs)]
    unnamed x140 -> x148, local copies, waits for them, and re-layouts: 80.5 us -> 11.6 us
    unnamed x8 -> x4, other arithmetic: 71.4 us -> 3.04 us
    pallas_call x0 -> x4, Pallas kernels: none -> 65.1 us  [the longest x2 41 us: attend_backward(): pl.pallas_call(functools.partial(backward_kernel, shards), grid=(images,...]
    all_gather x3 -> x0, blocking collectives: 59.9 us -> none  [the longest x1 23.2 us: per_device(): lax.all_gather(gains, 'dp', axis=0, tiled=True)]
  transfers between devices with their start and end apart: 19 -> 17, of which waited for: 8 -> 11; matrix products, arithmetic and copies ran while one was open for 44% -> 25% of each run, Pallas kernels for 0% -> 11%
where the time goes in v1:
time: 605 us; the launch traced here: 598 us
  waiting for transfers between devices  338 us (56%)
  matrix products  99.9 us (17%)
  Pallas kernels  65.1 us (11%)
  local copies, waits for them, and re-layouts  38.7 us (6%)
  other arithmetic  26.6 us (4%)
  between operations  15.8 us (3%)
  starting transfers between devices  13.1 us (2%)
    all_gather x1, waiting for transfers between devices, per_device(): full_out_up = gather(out_up)  89.3 us
    reduce_scatter x1, waiting for transfers between devices, per_device(): piece_qkvs = scatter(grad_qkvs)  71.8 us
    dot_general x8, matrix products, dot_f32(): lax.dot_general(a, b, (dims, ((), ())), preferred_element_type=jnp.float32)  66.2 us
    all_gather x1, waiting for transfers between devices, per_device(): full_qkvs = gather(jnp.concatenate([w_qkv, smalls], axis=1))  64.2 us
    ppermute x11, waiting for transfers between devices, shift(): lax.ppermute(values, 'seq', [(i, (i + step) % shards) for i in range(shar...  51.3 us
    reduce_scatter x1, waiting for transfers between devices, per_device(): piece_out_up = scatter(grad_out_up)  46.8 us
    pallas_call x2, Pallas kernels, attend_backward(): pl.pallas_call(functools.partial(backward_kernel, shards), grid=(images,...  41 us
    pallas_call x2, Pallas kernels, attend_forward(): pl.pallas_call(functools.partial(forward_kernel, shards), grid=(images, p...  24.1 us
  transfers between devices with their start and end apart: 17, of which 11 were waited for; matrix products, arithmetic and copies ran while one was open for 25% of the time, Pallas kernels for 11%

profile of v1, /device:TPU:0, one launch (start us, length us, event | category | flops | bytes accessed | tf_op | source)
XLA Modules:
  0.0 597.6 jit_solution(1756456433900639370)
XLA Ops:
  12.8 64.2 %all-gather.4.cloned.1.call-done = bf16[1024,3200]{1,0:T(8,128)(2,1)} async-done(((bf16[64,3200]{1,0:T(8,128)(2,1)}), bf16[1024,3200]{1,0:T(8,128)(2,1)}) %all-gather.4.cloned.1.call-update) | async-done | bytes 6553616 | tf_op jit(solution)/shard_map/all_gather | solution.py:165
  77.1 89.3 %all-gather.6.cloned.1.call-done = bf16[1024,5120]{1,0:T(8,128)(2,1)} async-done(((bf16[64,5120]{1,0:T(8,128)(2,1)}), bf16[1024,5120]{1,0:T(8,128)(2,1)}) %all-gather.6.cloned.1.call-update) | async-done | bytes 10485776 | tf_op jit(solution)/shard_map/all_gather | solution.py:168
  193.3 8.6 %collective-permute-done.1.refs_3_ = bf16[576,512]{1,0:T(8,128)(2,1)} collective-permute-done((bf16[576,512]{1,0:T(8,128)(2,1)}, bf16[576,512]{1,0:T(8,128)(2,1)}, u32[]{:S(2)}, u32[]{:S(2)}) %collective-permute-start.1) | collective-permute-done | bytes 589856 | tf_op jit(solution)/shard_map/ppermute | solution.py:147
  201.9 12.6 %shard_map.169 = (bf16[576,512]{1,0:T(8,128)(2,1)S(1)}, f32[1,4,2,576]{3,2,1,0:T(2,128)S(1)}) custom-call(s32[1]{0:T(128)} %bitcast.1.place_ref, s32[1]{0:T(128)S(6)} %copy.63.valid_ref, bf16[576,512]{1,0:T(8,128)(2,1)S(1)} %fusion.38.q_ref, bf16[576,512]{1,0:T(8,128)(2,1)S(1)} %convolution_convert_fusion.5.refs_0_, ...), custom_call_target="tpu_custom_call" | custom-call | flops 2717908992 | bytes 3538944 | tf_op jit(solution)/shard_map/pallas_call | solution.py:108
  214.7 11.8 %collective-permute-done.3.refs_3_ = bf16[576,512]{1,0:T(8,128)(2,1)S(1)} collective-permute-done((bf16[576,512]{1,0:T(8,128)(2,1)S(1)}, bf16[576,512]{1,0:T(8,128)(2,1)S(1)}, u32[]{:S(2)}, u32[]{:S(2)}) %collective-permute-start.3) | collective-permute-done | bytes 589856 | tf_op jit(solution)/shard_map/ppermute | solution.py:147
  226.4 11.5 %shard_map.170 = (bf16[576,512]{1,0:T(8,128)(2,1)S(1)}, f32[1,4,2,576]{3,2,1,0:T(2,128)S(1)}) custom-call(s32[1]{0:T(128)} %bitcast.1.place_ref, s32[1]{0:T(128)S(6)} %copy.63.valid_ref, bf16[576,512]{1,0:T(8,128)(2,1)S(1)} %fusion.40.q_ref, bf16[576,512]{1,0:T(8,128)(2,1)S(1)} %convolution_convert_fusion.4.refs_0_, ...), custom_call_target="tpu_custom_call" | custom-call | flops 2717908992 | bytes 3538944 | tf_op jit(solution)/shard_map/pallas_call | solution.py:108
  240.4 8.5 %multiply_convert_fusion = (bf16[576,4096]{1,0:T(8,128)(2,1)S(1)}, f32[576,4096]{1,0:T(8,128)}) fusion(f32[4096]{0:T(1024)S(1)} %copy-done.55, bf16[1024,5120]{1,0:T(8,128)(2,1)S(1)} %bitcast.77, f32[576,1024]{1,0:T(8,128)S(1)} %get-tuple-element.127, f32[1024]{0:T(1024)S(1)} %copy-done.60, f32[1024]{0:T(1024)S(1)} %copy-done.49, f32[576]{0:T(1024)S(1)} %fusion.55, ...), kind=kOutput, calls=%fused_computation.11 | convolution fusion | flops 4848943104 | bytes 24936448 | tf_op jit(solution)/shard_map/dot_general | solution.py:208
  251.2 9.0 %convolution_convert_fusion.1 = bf16[4096,1024]{1,0:T(8,128)(2,1)} fusion(bf16[576,4096]{1,0:T(8,128)(2,1)S(1)} %get-tuple-element.42, bf16[1,576,1024]{2,1,0:T(8,128)(2,1)S(1)} %copy-done.18), kind=kOutput, calls=%fused_computation.14 | convolution fusion | flops 4836032512 | bytes 14286848 | tf_op jit(solution)/shard_map/dot_general | solution.py:26
  260.3 13.3 %fusion.70 = (bf16[4096]{0:T(1024)(128)(2,1)}, bf16[576,4096]{1,0:T(8,128)(2,1)S(1)}) fusion(f32[576,4096]{1,0:T(8,128)} %get-tuple-element.129, f32[4096]{0:T(1024)} %add.186, bf16[4096,1024]{1,0:T(8,128)(2,1)} %all-gather.8.cloned.1.call-done, bf16[1,576,1024]{2,1,0:T(8,128)(2,1)S(1)} %copy-done.18), kind=kOutput, calls=%fused_computation.123 | convolution fusion | flops 4864864256 | bytes 23748608 | tf_op jit(solution)/shard_map/dot_general | solution.py:26
  273.7 10.8 %multiply_reduce_fusion = (bf16[1024]{0:T(1024)(128)(2,1)}, f32[576]{0:T(1024)S(1)}, bf16[1024]{0:T(1024)(128)(2,1)}, f32[576,1024]{1,0:T(8,128)S(1)}) fusion(f32[576,1024]{1,0:T(8,128)S(1)} %copy-done.21, f32[576]{0:T(1024)S(1)} %copy-done.53, f32[576]{0:T(1024)S(1)} %broadcast_multiply_fusion, f32[1024]{0:T(1024)S(1)} %copy-done.50, ...), kind=kOutput, calls=%fused_computation.40 | convolution fusion | flops 4836554240 | bytes 17840896 | tf_op jit(solution)/shard_map/dot_general | solution.py:26
  294.9 4.5 fusion.31
  299.4 10.0 %convolution_convert_fusion = bf16[1024,4096]{1,0:T(8,128)(2,1)S(1)} fusion(bf16[576,4096]{1,0:T(8,128)(2,1)} %copy-done.66, f32[576,1024]{1,0:T(8,128)S(1)} %copy-done.22, f32[1024]{0:T(1024)S(1)} %copy-done.61, f32[1024]{0:T(1024)S(1)} %copy-done.51, f32[576]{0:T(1024)S(1)} %copy-done.54, f32[576]{0:T(1024)S(1)} %broadcast_multiply_fusion), kind=kOutput, calls=%fused_computation.13 | convolution fusion | flops 4838981632 | bytes 15479296 | tf_op jit(solution)/shard_map/dot_general | solution.py:26
  309.4 4.8 pad_maximum_fusion
  320.7 20.8 %shard_map.171 = (bf16[576,512]{1,0:T(8,128)(2,1)S(1)}, f32[576,512]{1,0:T(8,128)}, bf16[576,512]{1,0:T(8,128)(2,1)}, f32[576,512]{1,0:T(8,128)}, bf16[576,512]{1,0:T(8,128)(2,1)}) custom-call(s32[1]{0:T(128)} %bitcast.1.place_ref, s32[1]{0:T(128)S(6)} %copy.63.valid_ref, bf16[576,512]{1,0:T(8,128)(2,1)S(1)} %copy-done.7, bf16[576,512]{1,0:T(8,128)(2,1)S(1)} %copy-done.1, ...), custom_call_target="tpu_custom_call" | custom-call | flops 6794772480 | bytes 7667712 | tf_op jit(solution)/shard_map/pallas_call | solution.py:132
  348.2 15.0 %reduce-scatter.4.cloned.1.call-done = bf16[256,1024]{1,0:T(8,128)(2,1)} async-done(((bf16[4096,1024]{1,0:T(8,128)(2,1)}), bf16[256,1024]{1,0:T(8,128)(2,1)}) %reduce-scatter.4.cloned.1.call-update) | async-done | bytes 524304 | tf_op jit(solution)/shard_map/reduce_scatter | solution.py:217
  365.0 20.2 %shard_map.172 = (bf16[576,512]{1,0:T(8,128)(2,1)S(1)}, f32[576,512]{1,0:T(8,128)}, bf16[576,512]{1,0:T(8,128)(2,1)S(1)}, f32[576,512]{1,0:T(8,128)}, bf16[576,512]{1,0:T(8,128)(2,1)S(1)}) custom-call(s32[1]{0:T(128)} %bitcast.1.place_ref, s32[1]{0:T(128)S(6)} %copy.63.valid_ref, bf16[576,512]{1,0:T(8,128)(2,1)S(1)} %copy-done.5, ...), custom_call_target="tpu_custom_call" | custom-call | flops 6794772480 | bytes 7667712 | tf_op jit(solution)/shard_map/pallas_call | solution.py:132
  389.3 12.1 %collective-permute-done.5 = bf16[576,512]{1,0:T(8,128)(2,1)S(1)} collective-permute-done((bf16[576,512]{1,0:T(8,128)(2,1)S(1)}, bf16[576,512]{1,0:T(8,128)(2,1)S(1)}, u32[]{:S(2)}, u32[]{:S(2)}) %collective-permute-start.5) | collective-permute-done | bytes 589856 | tf_op jit(solution)/shard_map/ppermute | solution.py:147
  403.0 9.9 %collective-permute-done.7 = bf16[576,512]{1,0:T(8,128)(2,1)S(1)} collective-permute-done((bf16[576,512]{1,0:T(8,128)(2,1)S(1)}, bf16[576,512]{1,0:T(8,128)(2,1)S(1)}, u32[]{:S(2)}, u32[]{:S(2)}) %collective-permute-start.7) | collective-permute-done | bytes 589856 | tf_op jit(solution)/shard_map/ppermute | solution.py:147
  413.2 7.5 %fusion.64 = (bf16[1024]{0:T(1024)(128)(2,1)S(1)}, f32[576]{0:T(1024)S(1)}, f32[576,1024]{1,0:T(8,128)S(1)}) fusion(f32[1024]{0:T(1024)S(1)} %copy-done.43, f32[576]{0:T(1024)S(1)} %broadcast_multiply_fusion.1, bf16[1,576,1024]{2,1,0:T(8,128)(2,1)S(1)} %copy-done.17, bf16[576,3072]{1,0:T(8,128)(2,1)S(1)} %get-tuple-element.118, ...), kind=kOutput, calls=%fused_computation.118 | convolution fusion | flops 3627416064 | bytes 13380096 | tf_op jit(solution)/shard_map/dot_general | solution.py:26
  428.3 7.8 %convolution_convert_fusion.2 = bf16[1024,3072]{1,0:T(8,128)(2,1)S(1)} fusion(bf16[576,3072]{1,0:T(8,128)(2,1)} %copy-done.41, bf16[1,576,1024]{2,1,0:T(8,128)(2,1)S(1)} %copy-done.17, f32[1024]{0:T(1024)} %copy-done.58, f32[1024]{0:T(1024)S(1)} %copy-done.43, f32[576]{0:T(1024)S(1)} %copy-done.48, f32[576]{0:T(1024)S(1)} %broadcast_multiply_fusion.1), kind=kOutput, calls=%fused_computation.22 | convolution fusion | flops 3630563328 | bytes 11022848 | tf_op jit(solution)/shard_map/dot_general | solution.py:26
  439.1 46.8 %reduce-scatter.6.cloned.1.call-done = bf16[64,5120]{1,0:T(8,128)(2,1)} async-done(((bf16[1024,5120]{1,0:T(8,128)(2,1)}), bf16[64,5120]{1,0:T(8,128)(2,1)}) %reduce-scatter.6.cloned.1.call-update) | async-done | bytes 655376 | tf_op jit(solution)/shard_map/reduce_scatter | solution.py:230
  487.5 9.8 %fusion.37 = bf16[1,576,1024]{2,1,0:T(8,128)(2,1)} fusion(f32[576,1024]{1,0:T(8,128)S(1)} %copy-done.23, bf16[576,4096]{1,0:T(8,128)(2,1)} %copy-done.67, bf16[4096,1024]{1,0:T(8,128)(2,1)} %all-gather.8.cloned.1.call-done, f32[1024]{0:T(1024)} %get-tuple-element.106), kind=kOutput, calls=%fused_computation.58 | convolution fusion | flops 4833607680 | bytes 16650240 | tf_op jit(solution)/shard_map/dot_general | solution.py:270
  504.6 71.8 %reduce-scatter.8.cloned.1.call-done = bf16[64,3200]{1,0:T(8,128)(2,1)} async-done(((bf16[1024,3200]{1,0:T(8,128)(2,1)}), bf16[64,3200]{1,0:T(8,128)(2,1)}) %reduce-scatter.8.cloned.1.call-update) | async-done | bytes 409616 | tf_op jit(solution)/shard_map/reduce_scatter | solution.py:268
  580.9 6.5 %collective-permute-done.8 = bf16[64,3200]{1,0:T(8,128)(2,1)S(1)} collective-permute-done((bf16[64,3200]{1,0:T(8,128)(2,1)}, bf16[64,3200]{1,0:T(8,128)(2,1)S(1)}, u32[]{:S(2)}, u32[]{:S(2)}) %collective-permute-start.8) | collective-permute-done | bytes 409632 | tf_op jit(solution)/shard_map/ppermute | solution.py:147
  (243 shorter events, 94.7 us)
Async XLA Ops:
  7.2 159.9 %copy-start.14 = (bf16[1,576,1024]{2,1,0:T(8,128)(2,1)S(1)}, bf16[1,576,1024]{2,1,0:T(8,128)(2,1)}, u32[]{:S(2)}) copy-start(bf16[1,576,1024]{2,1,0:T(8,128)(2,1)} %param.10) | copy-start | bytes 3538948
  7.2 69.9 %all-gather.4.cloned.1.call-start = ((), (), s32[]{:S(2)}) async-start(), calls=%async_computation.3 | async-start | bytes 6963200 | tf_op jit(solution)/shard_map/all_gather | solution.py:165
  10.8 155.6 %all-gather.6.cloned.1.call-start = ((), (), s32[]{:S(2)}) async-start(), calls=%async_computation.4 | async-start | bytes 11141120 | tf_op jit(solution)/shard_map/all_gather | solution.py:168
  77.1 183.1 %all-gather.8.cloned.1.call-start = ((), (), s32[]{:S(2)}) async-start(), calls=%async_computation.5 | async-start | bytes 8912896 | tf_op jit(solution)/shard_map/all_gather | solution.py:170
  166.4 196.8 %reduce-scatter.4.cloned.1.call-start = ((), (), s32[]{:S(2)}) async-start(), calls=%async_computation.6 | async-start | bytes 8912896 | tf_op jit(solution)/shard_map/reduce_scatter | solution.py:217
  172.9 29.0 %copy-start = (bf16[576,512]{1,0:T(8,128)(2,1)}, bf16[576,512]{1,0:T(8,128)(2,1)S(1)}, u32[]{:S(2)}) copy-start(bf16[576,512]{1,0:T(8,128)(2,1)S(1)} %convolution_convert_fusion.5.refs_0_) | copy-start | bytes 1769476
  172.9 20.3 %collective-permute-start = (bf16[576,512]{1,0:T(8,128)(2,1)S(1)}, bf16[576,512]{1,0:T(8,128)(2,1)S(1)}, u32[]{:S(2)}, u32[]{:S(2)}) collective-permute-start(bf16[576,512]{1,0:T(8,128)(2,1)S(1)} %convolution_convert_fusion.5.refs_0_), channel_id=1, source_target_pairs={{0,1},{1,0},{2,3},{3,2},{4,5},{5,4},{6,7},{7,6},{8,9},{9,8},{10,11... | collective-permute-start | bytes 1769480 | tf_op jit(solution)/shard_map/ppermute | solution.py:147
  178.6 23.3 %collective-permute-start.1 = (bf16[576,512]{1,0:T(8,128)(2,1)}, bf16[576,512]{1,0:T(8,128)(2,1)}, u32[]{:S(2)}, u32[]{:S(2)}) collective-permute-start(bf16[576,512]{1,0:T(8,128)(2,1)} %fusion.39.refs_2_), channel_id=1, source_target_pairs={{0,1},{1,0},{2,3},{3,2},{4,5},{5,4},{6,7},{7,6},{8,9},{9,8},{10,11... | collective-permute-start | bytes 1769480 | tf_op jit(solution)/shard_map/ppermute | solution.py:147
  181.3 33.4 %collective-permute-start.2 = (bf16[576,512]{1,0:T(8,128)(2,1)S(1)}, bf16[576,512]{1,0:T(8,128)(2,1)S(1)}, u32[]{:S(2)}, u32[]{:S(2)}) collective-permute-start(bf16[576,512]{1,0:T(8,128)(2,1)S(1)} %convolution_convert_fusion.4.refs_0_), channel_id=1, source_target_pairs={{0,1},{1,0},{2,3},{3,2},{4,5},{5,4},{6,7},{7,6},{8,9},{9,8},{10,11... | collective-permute-start | bytes 1769480 | tf_op jit(solution)/shard_map/ppermute | solution.py:147
  184.8 41.6 %collective-permute-start.3 = (bf16[576,512]{1,0:T(8,128)(2,1)S(1)}, bf16[576,512]{1,0:T(8,128)(2,1)S(1)}, u32[]{:S(2)}, u32[]{:S(2)}) collective-permute-start(bf16[576,512]{1,0:T(8,128)(2,1)S(1)} %fusion.41.refs_2_), channel_id=1, source_target_pairs={{0,1},{1,0},{2,3},{3,2},{4,5},{5,4},{6,7},{7,6},{8,9},{9,8},{10,11... | collective-permute-start | bytes 1769480 | tf_op jit(solution)/shard_map/ppermute | solution.py:147
  193.2 33.2 %copy-start.4 = (bf16[576,512]{1,0:T(8,128)(2,1)}, bf16[576,512]{1,0:T(8,128)(2,1)S(1)}, u32[]{:S(2)}) copy-start(bf16[576,512]{1,0:T(8,128)(2,1)S(1)} %fusion.40.q_ref) | copy-start | bytes 1769476
  201.9 36.1 %slice-start = ((s8[10485760]{0:T(1024)(128)(4,1)}), s8[4194304]{0:T(1024)(128)(4,1)S(1)}, s32[]{:S(2)}) async-start(s8[10485760]{0:T(1024)(128)(4,1)} %bitcast.76), calls=%async_computation.9 | async-start | bytes 8388608
  201.9 36.1 %slice-start.1 = ((s8[10485760]{0:T(1024)(128)(4,1)}), s8[4194304]{0:T(1024)(128)(4,1)S(1)}, s32[]{:S(2)}) async-start(s8[10485760]{0:T(1024)(128)(4,1)} %bitcast.76), calls=%async_computation.10 | async-start | bytes 8388608
  260.2 225.7 %reduce-scatter.6.cloned.1.call-start = ((), (), s32[]{:S(2)}) async-start(), calls=%async_computation.7 | async-start | bytes 11141120 | tf_op jit(solution)/shard_map/reduce_scatter | solution.py:230
  314.2 262.2 %reduce-scatter.8.cloned.1.call-start = ((), (), s32[]{:S(2)}) async-start(), calls=%async_computation.8 | async-start | bytes 6963200 | tf_op jit(solution)/shard_map/reduce_scatter | solution.py:268
  320.7 24.6 %copy-start.63 = (bf16[1024]{0:T(1024)(128)(2,1)S(1)}, bf16[1024]{0:T(1024)(128)(2,1)}, u32[]{:S(2)}) copy-start(bf16[1024]{0:T(1024)(128)(2,1)} %get-tuple-element.103) | copy-start | bytes 6148
  341.5 45.9 %collective-permute-start.4 = (bf16[576,512]{1,0:T(8,128)(2,1)}, bf16[576,512]{1,0:T(8,128)(2,1)}, u32[]{:S(2)}, u32[]{:S(2)}) collective-permute-start(bf16[576,512]{1,0:T(8,128)(2,1)} %get-tuple-element.52), channel_id=1, source_target_pairs={{0,1},{1,0},{2,3},{3,2},{4,5},{5,4},{6,7},{7,6},{8,9},{9,8},{10,11... | collective-permute-start | bytes 1769480 | tf_op jit(solution)/shard_map/ppermute | solution.py:147
  342.9 58.7 %collective-permute-start.6 = (bf16[576,512]{1,0:T(8,128)(2,1)}, bf16[576,512]{1,0:T(8,128)(2,1)}, u32[]{:S(2)}, u32[]{:S(2)}) collective-permute-start(bf16[576,512]{1,0:T(8,128)(2,1)} %get-tuple-element.56), channel_id=1, source_target_pairs={{0,1},{1,0},{2,3},{3,2},{4,5},{5,4},{6,7},{7,6},{8,9},{9,8},{10,11... | collective-permute-start | bytes 1769480 | tf_op jit(solution)/shard_map/ppermute | solution.py:147
  385.2 16.2 %collective-permute-start.5 = (bf16[576,512]{1,0:T(8,128)(2,1)S(1)}, bf16[576,512]{1,0:T(8,128)(2,1)S(1)}, u32[]{:S(2)}, u32[]{:S(2)}) collective-permute-start(bf16[576,512]{1,0:T(8,128)(2,1)S(1)} %get-tuple-element.54), channel_id=1, source_target_pairs={{0,1},{1,0},{2,3},{3,2},{4,5},{5,4},{6,7},{7,6},{8,9},{9,8},{10,11... | collective-permute-start | bytes 1769480 | tf_op jit(solution)/shard_map/ppermute | solution.py:147
  386.7 26.2 %collective-permute-start.7 = (bf16[576,512]{1,0:T(8,128)(2,1)S(1)}, bf16[576,512]{1,0:T(8,128)(2,1)S(1)}, u32[]{:S(2)}, u32[]{:S(2)}) collective-permute-start(bf16[576,512]{1,0:T(8,128)(2,1)S(1)} %get-tuple-element.58), channel_id=1, source_target_pairs={{0,1},{1,0},{2,3},{3,2},{4,5},{5,4},{6,7},{7,6},{8,9},{9,8},{10,11... | collective-permute-start | bytes 1769480 | tf_op jit(solution)/shard_map/ppermute | solution.py:147
  439.1 48.3 %copy-start.23 = (f32[576,1024]{1,0:T(8,128)S(1)}, f32[576,1024]{1,0:T(8,128)}, u32[]{:S(2)}) copy-start(f32[576,1024]{1,0:T(8,128)} %copy-done.20) | copy-start | bytes 7077892
  485.9 13.8 %collective-permute-start.10 = (bf16[256,1024]{1,0:T(8,128)(2,1)}, bf16[256,1024]{1,0:T(8,128)(2,1)S(1)}, u32[]{:S(2)}, u32[]{:S(2)}) collective-permute-start(bf16[256,1024]{1,0:T(8,128)(2,1)} %reduce-scatter.4.cloned.1.call-done), channel_id=1, source_target_pairs={{0,1},{1,0},{2,3},{3,2},{4,5},{5,4},{6,7},{7,6},{8,9},{9,8},{10,11... | collective-permute-start | bytes 1572872 | tf_op jit(solution)/shard_map/ppermute | solution.py:147
  500.9 77.0 %collective-permute-start.9 = (bf16[64,5120]{1,0:T(8,128)(2,1)}, bf16[64,5120]{1,0:T(8,128)(2,1)S(1)}, u32[]{:S(2)}, u32[]{:S(2)}) collective-permute-start(bf16[64,5120]{1,0:T(8,128)(2,1)} %reduce-scatter.6.cloned.1.call-done), channel_id=1, source_target_pairs={{0,1},{1,0},{2,3},{3,2},{4,5},{5,4},{6,7},{7,6},{8,9},{9,8},{10,11... | collective-permute-start | bytes 1966088 | tf_op jit(solution)/shard_map/ppermute | solution.py:147
  576.4 10.9 %collective-permute-start.8 = (bf16[64,3200]{1,0:T(8,128)(2,1)}, bf16[64,3200]{1,0:T(8,128)(2,1)S(1)}, u32[]{:S(2)}, u32[]{:S(2)}) collective-permute-start(bf16[64,3200]{1,0:T(8,128)(2,1)} %reduce-scatter.8.cloned.1.call-done), channel_id=1, source_target_pairs={{0,1},{1,0},{2,3},{3,2},{4,5},{5,4},{6,7},{7,6},{8,9},{9,8},{10,11... | collective-permute-start | bytes 1228808 | tf_op jit(solution)/shard_map/ppermute | solution.py:147
  (64 other events, 536.5 us)
Sparse Core Ops, SparseCore 0:
  10.9 66.0 all-gather.3
  79.9 86.4 all-gather.5
  168.5 73.0 all-gather.7
  260.4 102.7 reduce-scatter.3
  367.1 118.8 reduce-scatter.5
  489.7 86.6 reduce-scatter.7

commit v2 on v1

--- a/solution.py
+++ b/solution.py
@@ -147,6 +147,30 @@
     return lax.ppermute(values, "seq", [(i, (i + step) % shards) for i in range(shards)])
 
 
+def exchange(values, size, bit):
+    return lax.ppermute(values, "dp", [(i, i ^ bit) for i in range(size)])
+
+
+def my_bit(bit):
+    return (lax.axis_index("dp") // bit) % 2
+
+
+def doubling_step(blocks, size, bit):
+    other = exchange(blocks, size, bit)
+    mine = jnp.stack([blocks, other], axis=1)
+    swapped = jnp.stack([other, blocks], axis=1)
+    both = jnp.where(my_bit(bit) == 1, swapped, mine)
+    return both.reshape((-1,) + blocks.shape[1:])
+
+
+def halving_step(blocks, size, bit):
+    halves = blocks.reshape((-1, 2) + blocks.shape[1:])
+    keep = lax.dynamic_index_in_dim(halves, my_bit(bit), 1, keepdims=False)
+    send = lax.dynamic_index_in_dim(halves, 1 - my_bit(bit), 1, keepdims=False)
+    other = exchange(send, size, bit)
+    return (keep.astype(jnp.float32) + other.astype(jnp.float32)).astype(jnp.bfloat16)
+
+
 def per_device(tokens, w_qkv, w_out, w_up, w_down, gains, biases, up_bias, valid, cotangent):
     images, local_len, width = tokens.shape
     shard_rows = w_qkv.shape[0]
@@ -164,10 +188,15 @@
     smalls = jnp.pad(smalls, ((0, 0), (0, SMALL - smalls.shape[1])))
     full_qkvs = gather(jnp.concatenate([w_qkv, smalls], axis=1))
     out_up = jnp.concatenate([w_out, w_up], axis=1)
-    out_up, full_qkvs = lax.optimization_barrier((out_up, full_qkvs))
+    size = lax.axis_size("dp")
+    bits = [2**j for j in range(size.bit_length() - 1)]
+    blocks_down = w_down[None]
+    for bit in reversed(bits[2:]):
+        blocks_down = doubling_step(blocks_down, size, bit)
+    out_up, full_qkvs, blocks_down = lax.optimization_barrier((out_up, full_qkvs, blocks_down))
     full_out_up = gather(out_up)
-    w_down, full_out_up = lax.optimization_barrier((w_down, full_out_up))
-    full_down = gather(w_down)
+    for bit in bits[1:2]:
+        blocks_down = doubling_step(blocks_down, size, bit)
 
     full_qkv = full_qkvs[:, : 3 * width]
     small = full_qkvs[:, 3 * width :].astype(jnp.float32).T
@@ -199,7 +228,12 @@
         values = [v] + [shift(v, shards, -j) for j in range(1, shards)]
         groups.append((q, keys, values))
     parts = [attend_forward(images, place, valid, *group) for group in groups]
-    merged = jnp.concatenate([part[0] for part in parts], axis=1)
+    lead, blocks_down = lax.optimization_barrier((parts[0][0], blocks_down))
+    for bit in bits[:1]:
+        blocks_down = doubling_step(blocks_down, size, bit)
+    full_down = blocks_down.reshape(-1, width)
+    merged = jnp.concatenate([lead] + [part[0] for part in parts[1:]], axis=1)
+    merged, full_down = lax.optimization_barrier((merged, full_down))
 
     branch = jnp.dot(merged, full_out, preferred_element_type=jnp.float32) + bias_out
     residual = flat_tokens + branch
@@ -214,7 +248,9 @@
     grad_output = cotangent.reshape(-1, width)
     grad_down = dot_f32(activated, grad_output, ((0,), (0,))).astype(jnp.bfloat16)
     grad_down, full_down, activated = lax.optimization_barrier((grad_down, full_down, activated))
-    piece_down = scatter(grad_down)
+    blocks_down = grad_down.reshape((size,) + w_down.shape)
+    for bit in bits[:1]:
+        blocks_down = halving_step(blocks_down, size, bit)
 
     grad_act = dot_f32(grad_output, full_down, ((1,), (1,)))
     grad_upward = (grad_act * slope.astype(jnp.float32)).astype(jnp.bfloat16)
@@ -234,7 +270,9 @@
         lo, hi = g * piece, (g + 1) * piece
         grads = grad_merged[:, lo:hi]
         if g == SPLITS - 1:
-            grads, piece_down = lax.optimization_barrier((grads, piece_down))
+            for bit in bits[1:2]:
+                blocks_down = halving_step(blocks_down, size, bit)
+            grads, blocks_down = lax.optimization_barrier((grads, blocks_down))
         dq, *rest = attend_backward(images, place, valid, *group, part[1], grads)
         dk, dv = rest[0], rest[shards]
         for j in range(1, shards):
@@ -265,6 +303,9 @@
     small_grads = jnp.pad(small_grads, ((0, 0), (0, SMALL - small_grads.shape[1])))
     grad_qkvs = jnp.concatenate([grad_qkv, small_grads.astype(jnp.bfloat16)], axis=1)
     grad_qkvs, piece_out_up = lax.optimization_barrier((grad_qkvs, piece_out_up))
+    for bit in bits[2:]:
+        blocks_down = halving_step(blocks_down, size, bit)
+    piece_down = blocks_down[0]
     piece_qkvs = scatter(grad_qkvs)
 
     output = residual + jnp.dot(activated, full_down, preferred_element_type=jnp.float32)

time: 605 us -> 620 us (1.025)
  waiting for transfers between devices: 338 us -> 281 us
  other arithmetic: 26.6 us -> 65 us
  starting transfers between devices: 13.1 us -> 33.8 us
  local copies, waits for them, and re-layouts: 38.7 us -> 55.8 us
    ppermute x0 -> x8, waiting for transfers between devices: none -> 199 us  [exchange(): return lax.ppermute(values, 'dp', [(i, i ^ bit) for i in range(size)])]
    all_gather x1, waiting for transfers between devices: 89.3 us -> 0.01 us  [per_device(): full_out_up = gather(out_up)]
    all_gather x1, waiting for transfers between devices: 64.2 us -> 0.01 us  [per_device(): full_qkvs = gather(jnp.concatenate([w_qkv, smalls], axis=1))]
    reduce_scatter x1, waiting for transfers between devices: 71.8 us -> 7.63 us  [per_device(): piece_qkvs = scatter(grad_qkvs)]
    reduce_scatter x1, waiting for transfers between devices: 46.8 us -> 0.01 us  [per_device(): piece_out_up = scatter(grad_out_up)]
    ppermute x11, waiting for transfers between devices: 51.3 us -> 74.2 us  [shift(): lax.ppermute(values, 'seq', [(i, (i + step) % shards) for i in range(shar...]
    ppermute x0 -> x8, starting transfers between devices: none -> 21.7 us  [exchange(): return lax.ppermute(values, 'dp', [(i, i ^ bit) for i in range(size)])]
    select_n x0 -> x5, other arithmetic: none -> 20.3 us  [doubling_step(): both = jnp.where(my_bit(bit) == 1, swapped, mine)]
  transfers between devices with their start and end apart: 17 -> 23, of which waited for: 11 -> 16; matrix products, arithmetic and copies ran while one was open for 25% -> 20% of each run, Pallas kernels for 11% -> 11%
where the time goes in v2:
time: 620 us; the launch traced here: 614 us
  waiting for transfers between devices  281 us (45%)
  matrix products  97.4 us (16%)
  Pallas kernels  65.2 us (11%)
  other arithmetic  65 us (10%)
  local copies, waits for them, and re-layouts  55.8 us (9%)
  starting transfers between devices  33.8 us (5%)
  between operations  15.4 us (2%)
    ppermute x8, waiting for transfers between devices, exchange(): return lax.ppermute(values, 'dp', [(i, i ^ bit) for i in range(size)])  199 us
    ppermute x11, waiting for transfers between devices, shift(): lax.ppermute(values, 'seq', [(i, (i + step) % shards) for i in range(shar...  74.2 us
    dot_general x8, matrix products, dot_f32(): lax.dot_general(a, b, (dims, ((), ())), preferred_element_type=jnp.float32)  61.1 us
    pallas_call x2, Pallas kernels, attend_backward(): pl.pallas_call(functools.partial(backward_kernel, shards), grid=(images,...  41.5 us
    pallas_call x2, Pallas kernels, attend_forward(): pl.pallas_call(functools.partial(forward_kernel, shards), grid=(images, p...  23.8 us
    ppermute x8, starting transfers between devices, exchange(): return lax.ppermute(values, 'dp', [(i, i ^ bit) for i in range(size)])  21.7 us
    select_n x5, other arithmetic, doubling_step(): both = jnp.where(my_bit(bit) == 1, swapped, mine)  20.3 us
    convert_element_type x3, other arithmetic, halving_step(): (keep.astype(jnp.float32) + other.astype(jnp.float32)).astype(jnp.bfloat16)  13.1 us
  transfers between devices with their start and end apart: 23, of which 16 were waited for; matrix products, arithmetic and copies ran while one was open for 20% of the time, Pallas kernels for 11%

profile of v2, /device:TPU:0, one launch (start us, length us, event | category | flops | bytes accessed | tf_op | source)
XLA Modules:
  0.0 613.8 jit_solution(17782910714989161553)
XLA Ops:
  15.0 36.5 %collective-permute-done = bf16[1,256,1024]{2,1,0:T(8,128)(2,1)S(1)} collective-permute-done((bf16[1,256,1024]{2,1,0:T(8,128)(2,1)}, bf16[1,256,1024]{2,1,0:T(8,128)(2,1)S(1)}, u32[]{:S(2)}, u32[]{:S(2)}) %collective-permute-start) | collective-permute-done | bytes 524320 | tf_op jit(solution)/shard_map/ppermute | solution.py:151
  56.0 47.7 %collective-permute-done.1 = bf16[2,256,1024]{2,1,0:T(8,128)(2,1)S(1)} collective-permute-done((bf16[2,256,1024]{2,1,0:T(8,128)(2,1)S(1)}, bf16[2,256,1024]{2,1,0:T(8,128)(2,1)S(1)}, u32[]{:S(2)}, u32[]{:S(2)}) %collective-permute-start.1) | collective-permute-done | bytes 1048608 | tf_op jit(solution)/shard_map/ppermute | solution.py:151
  120.7 8.1 %collective-permute-done.2.refs_1_ = bf16[576,512]{1,0:T(8,128)(2,1)S(1)} collective-permute-done((bf16[576,512]{1,0:T(8,128)(2,1)S(1)}, bf16[576,512]{1,0:T(8,128)(2,1)S(1)}, u32[]{:S(2)}, u32[]{:S(2)}) %collective-permute-start.2) | collective-permute-done | bytes 589856 | tf_op jit(solution)/shard_map/ppermute | solution.py:147
  128.8 10.2 %collective-permute-done.3.refs_3_ = bf16[576,512]{1,0:T(8,128)(2,1)S(1)} collective-permute-done((bf16[576,512]{1,0:T(8,128)(2,1)S(1)}, bf16[576,512]{1,0:T(8,128)(2,1)S(1)}, u32[]{:S(2)}, u32[]{:S(2)}) %collective-permute-start.3) | collective-permute-done | bytes 589856 | tf_op jit(solution)/shard_map/ppermute | solution.py:147
  139.0 11.6 %shard_map.169 = (bf16[576,512]{1,0:T(8,128)(2,1)S(1)}, f32[1,4,2,576]{3,2,1,0:T(2,128)S(1)}) custom-call(s32[1]{0:T(128)} %bitcast.1.place_ref, s32[1]{0:T(128)S(6)} %copy.83.valid_ref, bf16[576,512]{1,0:T(8,128)(2,1)S(1)} %fusion.41.q_ref, bf16[576,512]{1,0:T(8,128)(2,1)S(1)} %convolution_convert_fusion.5.refs_0_, ...), custom_call_target="tpu_custom_call" | custom-call | flops 2717908992 | bytes 3538944 | tf_op jit(solution)/shard_map/pallas_call | solution.py:108
  150.6 18.6 %collective-permute-done.4 = bf16[4,256,1024]{2,1,0:T(8,128)(2,1)} collective-permute-done((bf16[4,256,1024]{2,1,0:T(8,128)(2,1)}, bf16[4,256,1024]{2,1,0:T(8,128)(2,1)}, u32[]{:S(2)}, u32[]{:S(2)}) %collective-permute-start.4) | collective-permute-done | bytes 2097184 | tf_op jit(solution)/shard_map/ppermute | solution.py:151
  193.6 12.2 %collective-permute-done.6.refs_3_ = bf16[576,512]{1,0:T(8,128)(2,1)} collective-permute-done((bf16[576,512]{1,0:T(8,128)(2,1)}, bf16[576,512]{1,0:T(8,128)(2,1)}, u32[]{:S(2)}, u32[]{:S(2)}) %collective-permute-start.6) | collective-permute-done | bytes 589856 | tf_op jit(solution)/shard_map/ppermute | solution.py:147
  205.8 12.1 %shard_map.170 = (bf16[576,512]{1,0:T(8,128)(2,1)S(1)}, f32[1,4,2,576]{3,2,1,0:T(2,128)S(1)}) custom-call(s32[1]{0:T(128)} %bitcast.1.place_ref, s32[1]{0:T(128)S(6)} %copy.83.valid_ref, bf16[576,512]{1,0:T(8,128)(2,1)S(1)} %fusion.43.q_ref, bf16[576,512]{1,0:T(8,128)(2,1)S(1)} %convolution_convert_fusion.4.refs_0_, ...), custom_call_target="tpu_custom_call" | custom-call | flops 2717908992 | bytes 3538944 | tf_op jit(solution)/shard_map/pallas_call | solution.py:108
  219.1 11.2 %maximum_select_fusion = bf16[8,2,256,1024]{3,2,0,1:T(8,128)(2,1)} fusion(bf16[8,1,256,1024]{3,2,0,1:T(8,128)(2,1)} %bitcast.12, bf16[8,1,256,1024]{3,2,0,1:T(8,128)(2,1)} %bitcast.11, pred[]{:T(512)S(6)} %eq.28), kind=kLoop, calls=%fused_computation.13 | loop fusion | flops 12582912 | bytes 16777216 | tf_op jit(solution)/shard_map/jit(_where)/select_n | solution.py:162
  244.3 9.3 %multiply_convert_fusion = (bf16[576,4096]{1,0:T(8,128)(2,1)}, f32[576,4096]{1,0:T(8,128)}) fusion(f32[4096]{0:T(1024)S(1)} %copy-done.46, bf16[1024,5120]{1,0:T(8,128)(2,1)S(1)} %copy-done.56, f32[576,1024]{1,0:T(8,128)S(1)} %get-tuple-element.142, f32[1024]{0:T(1024)S(1)} %copy-done.51, f32[1024]{0:T(1024)S(1)} %get-tuple-element.123, ...), kind=kOutput, calls=%fused_computation.11 | convolution fusion | flops 4848943104 | bytes 24936448 | tf_op jit(solution)/shard_map/dot_general | solution.py:242
  253.5 11.5 %convolution_convert_fusion.1 = bf16[4096,1024]{1,0:T(8,128)(2,1)} fusion(bf16[576,4096]{1,0:T(8,128)(2,1)} %get-tuple-element.48, bf16[1,576,1024]{2,1,0:T(8,128)(2,1)S(1)} %copy-done.18), kind=kOutput, calls=%fused_computation.17 | convolution fusion | flops 4836032512 | bytes 14286848 | tf_op jit(solution)/shard_map/dot_general | solution.py:26
  265.1 11.8 %fusion.74 = (bf16[4096]{0:T(1024)(128)(2,1)}, bf16[576,4096]{1,0:T(8,128)(2,1)}) fusion(f32[576,4096]{1,0:T(8,128)} %get-tuple-element.144, f32[4096]{0:T(1024)S(1)} %copy-done.46, bf16[4096,1024]{1,0:T(8,128)(2,1)S(1)} %bitcast.116, bf16[1,576,1024]{2,1,0:T(8,128)(2,1)S(1)} %copy-done.18), kind=kOutput, calls=%fused_computation.139 | convolution fusion | flops 4864864256 | bytes 23748608 | tf_op jit(solution)/shard_map/dot_general | solution.py:26
  276.9 12.2 %convolution_convert_fusion = bf16[1024,4096]{1,0:T(8,128)(2,1)} fusion(bf16[576,4096]{1,0:T(8,128)(2,1)} %get-tuple-element.148, f32[576,1024]{1,0:T(8,128)S(1)} %get-tuple-element.142, f32[1024]{0:T(1024)S(1)} %copy-done.51, f32[1024]{0:T(1024)S(1)} %get-tuple-element.123, f32[576]{0:T(1024)S(1)} %fusion.59, f32[576]{0:T(1024)S(1)} %broadcast_multiply_fusion), kind=kOutput, calls=%fused_computation.16 | convolution fusion | flops 4838981632 | bytes 15479296 | tf_op jit(solution)/shard_map/dot_general | solution.py:26
  305.7 9.7 %pad_maximum_fusion = bf16[1024,5120]{1,0:T(8,128)(2,1)} fusion(bf16[1024,4096]{1,0:T(8,128)(2,1)} %convolution_convert_fusion, bf16[1024,1024]{1,0:T(8,128)(2,1)} %copy.64), kind=kLoop, calls=%fused_computation.3 | loop fusion | flops 20971520 | bytes 20971520 | tf_op jit(solution)/shard_map/concatenate | solution.py:264
  349.9 20.3 %shard_map.171 = (bf16[576,512]{1,0:T(8,128)(2,1)S(1)}, f32[576,512]{1,0:T(8,128)}, bf16[576,512]{1,0:T(8,128)(2,1)}, f32[576,512]{1,0:T(8,128)}, bf16[576,512]{1,0:T(8,128)(2,1)}) custom-call(s32[1]{0:T(128)} %bitcast.1.place_ref, s32[1]{0:T(128)S(6)} %copy.83.valid_ref, bf16[576,512]{1,0:T(8,128)(2,1)S(1)} %copy-done.3, ...), custom_call_target="tpu_custom_call" | custom-call | flops 6794772480 | bytes 7667712 | tf_op jit(solution)/shard_map/pallas_call | solution.py:132
  376.9 28.1 %collective-permute-done.9 = bf16[4,256,1024]{2,1,0:T(8,128)(2,1)} collective-permute-done((bf16[4,256,1024]{2,1,0:T(8,128)(2,1)}, bf16[4,256,1024]{2,1,0:T(8,128)(2,1)}, u32[]{:S(2)}, u32[]{:S(2)}) %collective-permute-start.9) | collective-permute-done | bytes 2097184 | tf_op jit(solution)/shard_map/ppermute | solution.py:151
  409.7 21.2 %shard_map.172 = (bf16[576,512]{1,0:T(8,128)(2,1)S(1)}, f32[576,512]{1,0:T(8,128)}, bf16[576,512]{1,0:T(8,128)(2,1)S(1)}, f32[576,512]{1,0:T(8,128)}, bf16[576,512]{1,0:T(8,128)(2,1)S(1)}) custom-call(s32[1]{0:T(128)} %bitcast.1.place_ref, s32[1]{0:T(128)S(6)} %copy.83.valid_ref, bf16[576,512]{1,0:T(8,128)(2,1)S(1)} %copy-done.5, ...), custom_call_target="tpu_custom_call" | custom-call | flops 6794772480 | bytes 7667712 | tf_op jit(solution)/shard_map/pallas_call | solution.py:132
  433.8 13.4 %collective-permute-done.11 = bf16[576,512]{1,0:T(8,128)(2,1)S(1)} collective-permute-done((bf16[576,512]{1,0:T(8,128)(2,1)S(1)}, bf16[576,512]{1,0:T(8,128)(2,1)S(1)}, u32[]{:S(2)}, u32[]{:S(2)}) %collective-permute-start.11) | collective-permute-done | bytes 589856 | tf_op jit(solution)/shard_map/ppermute | solution.py:147
  449.7 8.2 %collective-permute-done.13 = bf16[576,512]{1,0:T(8,128)(2,1)S(1)} collective-permute-done((bf16[576,512]{1,0:T(8,128)(2,1)S(1)}, bf16[576,512]{1,0:T(8,128)(2,1)S(1)}, u32[]{:S(2)}, u32[]{:S(2)}) %collective-permute-start.13) | collective-permute-done | bytes 589856 | tf_op jit(solution)/shard_map/ppermute | solution.py:147
  483.2 11.4 %collective-permute-start.16 = (bf16[2,256,1024]{2,1,0:T(8,128)(2,1)}, bf16[2,256,1024]{2,1,0:T(8,128)(2,1)}, u32[]{:S(2)}, u32[]{:S(2)}) collective-permute-start(bf16[2,256,1024]{2,1,0:T(8,128)(2,1)} %dynamic-slice_bitcast_fusion.2), channel_id=1, source_target_pairs={{0,8},{2,10},{4,12},{6,14},{8,0},{10,2},{12,4},{14,6},{16,24},{18,... | collective-permute-start | bytes 3145736 | tf_op jit(solution)/shard_map/ppermute | solution.py:151
  494.6 23.1 %collective-permute-done.16 = bf16[2,256,1024]{2,1,0:T(8,128)(2,1)} collective-permute-done((bf16[2,256,1024]{2,1,0:T(8,128)(2,1)}, bf16[2,256,1024]{2,1,0:T(8,128)(2,1)}, u32[]{:S(2)}, u32[]{:S(2)}) %collective-permute-start.16) | collective-permute-done | bytes 1048608 | tf_op jit(solution)/shard_map/ppermute | solution.py:151
  521.4 9.8 %fusion.40 = bf16[1,576,1024]{2,1,0:T(8,128)(2,1)} fusion(f32[576,1024]{1,0:T(8,128)S(1)} %copy-done.21, bf16[576,4096]{1,0:T(8,128)(2,1)} %get-tuple-element.48, bf16[4096,1024]{1,0:T(8,128)(2,1)} %bitcast.113, f32[1024]{0:T(1024)S(1)} %copy-done.48), kind=kOutput, calls=%fused_computation.69 | convolution fusion | flops 4833607680 | bytes 16650240 | tf_op jit(solution)/shard_map/dot_general | solution.py:311
  531.2 37.8 %collective-permute-done.17 = bf16[1,256,1024]{2,1,0:T(8,128)(2,1)S(1)} collective-permute-done((bf16[1,256,1024]{2,1,0:T(8,128)(2,1)S(1)}, bf16[1,256,1024]{2,1,0:T(8,128)(2,1)S(1)}, u32[]{:S(2)}, u32[]{:S(2)}) %collective-permute-start.17) | collective-permute-done | bytes 524320 | tf_op jit(solution)/shard_map/ppermute | solution.py:151
  573.5 10.6 %collective-permute-done.18 = bf16[256,1024]{1,0:T(8,128)(2,1)S(1)} collective-permute-done((bf16[256,1024]{1,0:T(8,128)(2,1)S(1)}, bf16[256,1024]{1,0:T(8,128)(2,1)S(1)}, u32[]{:S(2)}, u32[]{:S(2)}) %collective-permute-start.18) | collective-permute-done | bytes 524320 | tf_op jit(solution)/shard_map/ppermute | solution.py:147
  (249 shorter events, 191.8 us)
Async XLA Ops:
  7.2 98.1 %all-gather.3.cloned.1.call-start = ((), (), s32[]{:S(2)}) async-start(), calls=%async_computation.2 | async-start | bytes 6963200 | tf_op jit(solution)/shard_map/all_gather | solution.py:189
  10.8 227.6 %all-gather.5.cloned.1.call-start = ((), (), s32[]{:S(2)}) async-start(), calls=%async_computation.3 | async-start | bytes 11141120 | tf_op jit(solution)/shard_map/all_gather | solution.py:197
  10.9 40.6 %collective-permute-start = (bf16[1,256,1024]{2,1,0:T(8,128)(2,1)}, bf16[1,256,1024]{2,1,0:T(8,128)(2,1)S(1)}, u32[]{:S(2)}, u32[]{:S(2)}) collective-permute-start(bf16[1,256,1024]{2,1,0:T(8,128)(2,1)} %bitcast.119), channel_id=1, source_target_pairs={{0,16},{2,18},{4,20},{6,22},{8,24},{10,26},{12,28},{14,30},{16,0},... | collective-permute-start | bytes 1572872 | tf_op jit(solution)/shard_map/ppermute | solution.py:151
  52.9 50.7 %collective-permute-start.1 = (bf16[2,256,1024]{2,1,0:T(8,128)(2,1)S(1)}, bf16[2,256,1024]{2,1,0:T(8,128)(2,1)S(1)}, u32[]{:S(2)}, u32[]{:S(2)}) collective-permute-start(bf16[2,256,1024]{2,1,0:T(8,128)(2,1)S(1)} %maximum_select_fusion.3), channel_id=1, source_target_pairs={{0,8},{2,10},{4,12},{6,14},{8,0},{10,2},{12,4},{14,6},{16,24},{18,... | collective-permute-start | bytes 3145736 | tf_op jit(solution)/shard_map/ppermute | solution.py:151
  105.3 375.2 %reduce-scatter.3.cloned.1.call-start = ((), (), s32[]{:S(2)}) async-start(), calls=%async_computation.4 | async-start | bytes 11141120 | tf_op jit(solution)/shard_map/reduce_scatter | solution.py:266
  106.1 63.1 %collective-permute-start.4 = (bf16[4,256,1024]{2,1,0:T(8,128)(2,1)}, bf16[4,256,1024]{2,1,0:T(8,128)(2,1)}, u32[]{:S(2)}, u32[]{:S(2)}) collective-permute-start(bf16[4,256,1024]{2,1,0:T(8,128)(2,1)} %bitcast.6), channel_id=1, source_target_pairs={{0,4},{2,6},{4,0},{6,2},{8,12},{10,14},{12,8},{14,10},{16,20},{18,... | collective-permute-start | bytes 6291464 | tf_op jit(solution)/shard_map/ppermute | solution.py:151
  107.5 78.7 %copy-start.43 = (f32[576]{0:T(1024)}, f32[576]{0:T(1024)S(1)}, u32[]{:S(2)}) copy-start(f32[576]{0:T(1024)S(1)} %fusion.58) | copy-start | bytes 6916
  112.5 16.3 %collective-permute-start.2 = (bf16[576,512]{1,0:T(8,128)(2,1)S(1)}, bf16[576,512]{1,0:T(8,128)(2,1)S(1)}, u32[]{:S(2)}, u32[]{:S(2)}) collective-permute-start(bf16[576,512]{1,0:T(8,128)(2,1)S(1)} %convolution_convert_fusion.5.refs_0_), channel_id=1, source_target_pairs={{0,1},{1,0},{2,3},{3,2},{4,5},{5,4},{6,7},{7,6},{8,9},{9,8},{10,11... | collective-permute-start | bytes 1769480 | tf_op jit(solution)/shard_map/ppermute | solution.py:147
  117.4 21.5 %collective-permute-start.3 = (bf16[576,512]{1,0:T(8,128)(2,1)S(1)}, bf16[576,512]{1,0:T(8,128)(2,1)S(1)}, u32[]{:S(2)}, u32[]{:S(2)}) collective-permute-start(bf16[576,512]{1,0:T(8,128)(2,1)S(1)} %fusion.42.refs_2_), channel_id=1, source_target_pairs={{0,1},{1,0},{2,3},{3,2},{4,5},{5,4},{6,7},{7,6},{8,9},{9,8},{10,11... | collective-permute-start | bytes 1769480 | tf_op jit(solution)/shard_map/ppermute | solution.py:147
  175.1 44.0 %collective-permute-start.7 = (bf16[8,256,1024]{2,1,0:T(8,128)(2,1)}, bf16[8,256,1024]{2,1,0:T(8,128)(2,1)}, u32[]{:S(2)}, u32[]{:S(2)}) collective-permute-start(bf16[8,256,1024]{2,1,0:T(8,128)(2,1)} %bitcast.10), channel_id=1, source_target_pairs={{0,2},{2,0},{4,6},{6,4},{8,10},{10,8},{12,14},{14,12},{16,18},{18,... | collective-permute-start | bytes 12582920 | tf_op jit(solution)/shard_map/ppermute | solution.py:151
  177.3 16.3 %collective-permute-start.5 = (bf16[576,512]{1,0:T(8,128)(2,1)S(1)}, bf16[576,512]{1,0:T(8,128)(2,1)}, u32[]{:S(2)}, u32[]{:S(2)}) collective-permute-start(bf16[576,512]{1,0:T(8,128)(2,1)S(1)} %convolution_convert_fusion.4.refs_0_), channel_id=1, source_target_pairs={{0,1},{1,0},{2,3},{3,2},{4,5},{5,4},{6,7},{7,6},{8,9},{9,8},{10,11... | collective-permute-start | bytes 1769480 | tf_op jit(solution)/shard_map/ppermute | solution.py:147
  181.3 24.5 %collective-permute-start.6 = (bf16[576,512]{1,0:T(8,128)(2,1)}, bf16[576,512]{1,0:T(8,128)(2,1)}, u32[]{:S(2)}, u32[]{:S(2)}) collective-permute-start(bf16[576,512]{1,0:T(8,128)(2,1)} %fusion.44.refs_2_), channel_id=1, source_target_pairs={{0,1},{1,0},{2,3},{3,2},{4,5},{5,4},{6,7},{7,6},{8,9},{9,8},{10,11... | collective-permute-start | bytes 1769480 | tf_op jit(solution)/shard_map/ppermute | solution.py:147
  319.8 273.1 %reduce-scatter.5.cloned.1.call-start = ((), (), s32[]{:S(2)}) async-start(), calls=%async_computation.5 | async-start | bytes 6963200 | tf_op jit(solution)/shard_map/reduce_scatter | solution.py:309
  324.4 7.5 %collective-permute-start.8 = (bf16[8,256,1024]{2,1,0:T(8,128)(2,1)}, bf16[8,256,1024]{2,1,0:T(8,128)(2,1)}, u32[]{:S(2)}, u32[]{:S(2)}) collective-permute-start(bf16[8,256,1024]{2,1,0:T(8,128)(2,1)} %dynamic-slice_bitcast_fusion), channel_id=1, source_target_pairs={{0,2},{2,0},{4,6},{6,4},{8,10},{10,8},{12,14},{14,12},{16,18},{18,... | collective-permute-start | bytes 12582920 | tf_op jit(solution)/shard_map/ppermute | solution.py:151
  342.0 63.0 %collective-permute-start.9 = (bf16[4,256,1024]{2,1,0:T(8,128)(2,1)}, bf16[4,256,1024]{2,1,0:T(8,128)(2,1)}, u32[]{:S(2)}, u32[]{:S(2)}) collective-permute-start(bf16[4,256,1024]{2,1,0:T(8,128)(2,1)} %dynamic-slice_bitcast_fusion.1), channel_id=1, source_target_pairs={{0,4},{2,6},{4,0},{6,2},{8,12},{10,14},{12,8},{14,10},{16,20},{18,... | collective-permute-start | bytes 6291464 | tf_op jit(solution)/shard_map/ppermute | solution.py:151
  370.2 63.0 %collective-permute-start.10 = (bf16[576,512]{1,0:T(8,128)(2,1)}, bf16[576,512]{1,0:T(8,128)(2,1)S(1)}, u32[]{:S(2)}, u32[]{:S(2)}) collective-permute-start(bf16[576,512]{1,0:T(8,128)(2,1)} %get-tuple-element.58), channel_id=1, source_target_pairs={{0,1},{1,0},{2,3},{3,2},{4,5},{5,4},{6,7},{7,6},{8,9},{9,8},{10,11... | collective-permute-start | bytes 1769480 | tf_op jit(solution)/shard_map/ppermute | solution.py:147
  371.7 75.8 %collective-permute-start.12 = (bf16[576,512]{1,0:T(8,128)(2,1)}, bf16[576,512]{1,0:T(8,128)(2,1)S(1)}, u32[]{:S(2)}, u32[]{:S(2)}) collective-permute-start(bf16[576,512]{1,0:T(8,128)(2,1)} %get-tuple-element.62), channel_id=1, source_target_pairs={{0,1},{1,0},{2,3},{3,2},{4,5},{5,4},{6,7},{7,6},{8,9},{9,8},{10,11... | collective-permute-start | bytes 1769480 | tf_op jit(solution)/shard_map/ppermute | solution.py:147
  430.9 16.3 %collective-permute-start.11 = (bf16[576,512]{1,0:T(8,128)(2,1)S(1)}, bf16[576,512]{1,0:T(8,128)(2,1)S(1)}, u32[]{:S(2)}, u32[]{:S(2)}) collective-permute-start(bf16[576,512]{1,0:T(8,128)(2,1)S(1)} %get-tuple-element.60), channel_id=1, source_target_pairs={{0,1},{1,0},{2,3},{3,2},{4,5},{5,4},{6,7},{7,6},{8,9},{9,8},{10,11... | collective-permute-start | bytes 1769480 | tf_op jit(solution)/shard_map/ppermute | solution.py:147
  432.4 25.5 %collective-permute-start.13 = (bf16[576,512]{1,0:T(8,128)(2,1)S(1)}, bf16[576,512]{1,0:T(8,128)(2,1)S(1)}, u32[]{:S(2)}, u32[]{:S(2)}) collective-permute-start(bf16[576,512]{1,0:T(8,128)(2,1)S(1)} %get-tuple-element.64), channel_id=1, source_target_pairs={{0,1},{1,0},{2,3},{3,2},{4,5},{5,4},{6,7},{7,6},{8,9},{9,8},{10,11... | collective-permute-start | bytes 1769480 | tf_op jit(solution)/shard_map/ppermute | solution.py:147
  483.2 34.5 %collective-permute-start.16 = (bf16[2,256,1024]{2,1,0:T(8,128)(2,1)}, bf16[2,256,1024]{2,1,0:T(8,128)(2,1)}, u32[]{:S(2)}, u32[]{:S(2)}) collective-permute-start(bf16[2,256,1024]{2,1,0:T(8,128)(2,1)} %dynamic-slice_bitcast_fusion.2), channel_id=1, source_target_pairs={{0,8},{2,10},{4,12},{6,14},{8,0},{10,2},{12,4},{14,6},{16,24},{18,... | collective-permute-start | bytes 3145736 | tf_op jit(solution)/shard_map/ppermute | solution.py:151
  519.7 49.3 %collective-permute-start.17 = (bf16[1,256,1024]{2,1,0:T(8,128)(2,1)S(1)}, bf16[1,256,1024]{2,1,0:T(8,128)(2,1)S(1)}, u32[]{:S(2)}, u32[]{:S(2)}) collective-permute-start(bf16[1,256,1024]{2,1,0:T(8,128)(2,1)S(1)} %constant_dynamic-slice_fusion), channel_id=1, source_target_pairs={{0,16},{2,18},{4,20},{6,22},{8,24},{10,26},{12,28},{14,30},{16,0},... | collective-permute-start | bytes 1572872 | tf_op jit(solution)/shard_map/ppermute | solution.py:151
  569.2 14.9 %collective-permute-start.18 = (bf16[256,1024]{1,0:T(8,128)(2,1)S(1)}, bf16[256,1024]{1,0:T(8,128)(2,1)S(1)}, u32[]{:S(2)}, u32[]{:S(2)}) collective-permute-start(bf16[256,1024]{1,0:T(8,128)(2,1)S(1)} %fusion.56), channel_id=1, source_target_pairs={{0,1},{1,0},{2,3},{3,2},{4,5},{5,4},{6,7},{7,6},{8,9},{9,8},{10,11... | collective-permute-start | bytes 1572872 | tf_op jit(solution)/shard_map/ppermute | solution.py:147
  571.0 23.4 %collective-permute-start.15 = (bf16[64,5120]{1,0:T(8,128)(2,1)}, bf16[64,5120]{1,0:T(8,128)(2,1)S(1)}, u32[]{:S(2)}, u32[]{:S(2)}) collective-permute-start(bf16[64,5120]{1,0:T(8,128)(2,1)} %reduce-scatter.3.cloned.1.call-done), channel_id=1, source_target_pairs={{0,1},{1,0},{2,3},{3,2},{4,5},{5,4},{6,7},{7,6},{8,9},{9,8},{10,11... | collective-permute-start | bytes 1966088 | tf_op jit(solution)/shard_map/ppermute | solution.py:147
  592.9 11.0 %collective-permute-start.14 = (bf16[64,3200]{1,0:T(8,128)(2,1)}, bf16[64,3200]{1,0:T(8,128)(2,1)S(1)}, u32[]{:S(2)}, u32[]{:S(2)}) collective-permute-start(bf16[64,3200]{1,0:T(8,128)(2,1)} %reduce-scatter.5.cloned.1.call-done), channel_id=1, source_target_pairs={{0,1},{1,0},{2,3},{3,2},{4,5},{5,4},{6,7},{7,6},{8,9},{9,8},{10,11... | collective-permute-start | bytes 1228808 | tf_op jit(solution)/shard_map/ppermute | solution.py:147
  (61 other events, 1037.3 us)
Sparse Core Ops, SparseCore 0:
  10.9 91.7 all-gather.2
  105.6 104.4 all-gather.4
  319.9 138.8 reduce-scatter.2
  480.7 112.1 reduce-scatter.4
